TPU v7x, 512 devices: a whole 4x4x16 slice. The times are simulated.
512 devices in a mesh: gy: 32 (over x, y, core), gz: 16 (over z).
Axes of the slice: x: 4, y: 4, z: 16, core: 2. Of those that a mesh axis runs over, the one named last changes fastest.
Arguments:
- volume: bfloat16 [64, 128, 64, 256], P(None, 'gy', 'gz'), may hold values from -2500 to 2500
- down_weight: bfloat16 [128, 64, 2, 2, 2], replicated, may hold values from -0.25 to 0.25
- conv_one: bfloat16 [3, 3, 128, 384], replicated, may hold values from -0.109375 to 0.109375
- conv_two: bfloat16 [3, 3, 128, 384], replicated, may hold values from -0.109375 to 0.109375
- norm_gain: float32 [3, 128], replicated, may hold values from 0.1 to 1.9
- norm_shift: float32 [3, 128], replicated, may hold values from -2.5 to 2.5
Outputs:
- features: bfloat16 [128, 64, 32, 128], P(None, 'gy', 'gz')
All inputs are finite; a program needn't handle non-finite values.
Results may differ from a plain program's by a relative error of at most 0.0065.
Values may be sent and summed in bfloat16 or wider, within the bound.
No kernel may reach another device: no remote copies, remote signals or barrier semaphores. Data moves between devices by JAX's collectives and lax.ppermute only.
A program may use at most 64 MiB of HBM per device.

v0:
```python
import jax
import jax.numpy as jnp
from jax import lax
from jax.sharding import PartitionSpec as P


def padded_2(value, sides, width):
    for axis, dim in sides:
        count, length = (lax.axis_size(axis), value.shape[dim])
        up = [(i, (i + 1) % count) for i in range(count - 1)]
        down = [(j, i) for i, j in up]
        last = lax.slice_in_dim(value, length - width, length, axis=dim)
        leading = lax.slice_in_dim(value, 0, width, axis=dim)
        before = lax.ppermute(last, axis, up)
        after = lax.ppermute(leading, axis, down)
        value = jnp.concatenate([before, value, after], axis=dim)
    return value


def leaky(value):
    return jnp.where(value >= 0.0, value, 0.01 * value)


def moments(inner):
    count = float(
        inner.shape[1] * inner.shape[2] * inner.shape[3] * lax.axis_size("gy") * lax.axis_size("gz")
    )
    total = lax.psum(jnp.sum(inner, axis=(1, 2, 3)), ("gy", "gz"))
    mean = total / count
    centered = inner - mean[:, None, None, None]
    spread = lax.psum(jnp.sum(centered * centered, axis=(1, 2, 3)), ("gy", "gz")) / count
    return (mean, spread)


def normalize(value, inner, gain, shift):
    mean, spread = moments(inner)
    scaled = (value - mean[:, None, None, None]) / jnp.sqrt(spread + 1e-05)[:, None, None, None]
    return leaky(scaled * gain[:, None, None, None] + shift[:, None, None, None])


def strided(volume, down_weight):
    blocks = volume.reshape(
        volume.shape[0], volume.shape[1] // 2, 2, volume.shape[2] // 2, 2, volume.shape[3] // 2, 2
    )
    return jnp.einsum(
        "oiabc,iyazbxc->oyzx", down_weight, blocks, preferred_element_type=jnp.float32
    )


def convolve(padded, conv_weight, rows, depth):
    length = padded.shape[3]
    widened = jnp.pad(padded, ((0, 0), (0, 0), (0, 0), (1, 1)))
    stacked = jnp.concatenate(
        [widened[:, :, :, offset : offset + length] for offset in range(3)], axis=0
    )
    total = jnp.zeros((conv_weight.shape[2], rows, depth, length), jnp.float32)
    for row_tap in range(3):
        for depth_tap in range(3):
            piece = stacked[:, row_tap : row_tap + rows, depth_tap : depth_tap + depth, :]
            total = total + jnp.einsum(
                "ok,kyzx->oyzx",
                conv_weight[row_tap, depth_tap],
                piece,
                preferred_element_type=jnp.float32,
            )
    return total


def faces(field):
    return padded_2(field, (("gy", 1), ("gz", 2)), 1)


def on_device(volume, down_weight, conv_one, conv_two, norm_gain, norm_shift):
    coarse = strided(volume, down_weight)
    rows = coarse.shape[1]
    depth = coarse.shape[2]
    first = normalize(coarse, coarse, norm_gain[0], norm_shift[0]).astype(jnp.bfloat16)
    middle = convolve(faces(first), conv_one, rows, depth)
    second = normalize(middle, middle, norm_gain[1], norm_shift[1]).astype(jnp.bfloat16)
    last = convolve(faces(second), conv_two, rows, depth)
    return normalize(last, last, norm_gain[2], norm_shift[2]).astype(jnp.bfloat16)


def solution(mesh):
    return jax.shard_map(
        on_device,
        mesh=mesh,
        in_specs=(P(None, "gy", "gz", None), P(), P(), P(), P(), P()),
        out_specs=P(None, "gy", "gz", None),
        check_vma=False,
    )
```

profile of v0, /device:TPU:1, one launch (start us, length us, event | category | flops | bytes accessed | tf_op | source)
XLA Modules:
  0.0 662.0 jit_solution(10334304953308035063)
XLA Ops:
  0.0 1.7 copy.10
  2.1 111.0 %psum.42 = f32[128]{0:T(128)S(1)} all-reduce(f32[128]{0:T(128)S(1)} %get-tuple-element.23), channel_id=1, replica_groups=mesh['gy'=32,'gz'=16] {'gy','gz'}, use_global_device_ids=true, to_apply=%region_1.0 | all-reduce | flops 128 | bytes 1024 | tf_op jit(solution)/shard_map/psum | solution.py:28
  113.2 98.2 %psum.43 = f32[128]{0:T(128)S(1)} all-reduce(f32[128]{0:T(128)S(1)} %multiply_reduce_fusion.2), channel_id=1, replica_groups=mesh['gy'=32,'gz'=16] {'gy','gz'}, use_global_device_ids=true, to_apply=%region_3.0 | all-reduce | flops 128 | bytes 1024 | tf_op jit(solution)/shard_map/psum | solution.py:31
  211.6 2.9 collective-permute-start
  214.5 1.9 collective-permute-start.1
  216.4 3.6 collective-permute-done.1
  220.1 3.7 collective-permute-start.2
  223.8 1.3 collective-permute-start.3
  225.1 0.6 collective-permute-done.2
  225.7 3.8 collective-permute-done.3
  230.2 0.9 copy-done
  233.6 102.8 %psum.44 = f32[128]{0:T(128)S(1)} all-reduce(f32[128]{0:T(128)S(1)} %get-tuple-element.25), channel_id=1, replica_groups=mesh['gy'=32,'gz'=16] {'gy','gz'}, use_global_device_ids=true, to_apply=%region_5.6 | all-reduce | flops 128 | bytes 1024 | tf_op jit(solution)/shard_map/psum | solution.py:28
  336.5 99.5 %psum.45 = f32[128]{0:T(128)S(1)} all-reduce(f32[128]{0:T(128)S(1)} %multiply_reduce_fusion.1), channel_id=1, replica_groups=mesh['gy'=32,'gz'=16] {'gy','gz'}, use_global_device_ids=true, to_apply=%region_7.8 | all-reduce | flops 128 | bytes 1024 | tf_op jit(solution)/shard_map/psum | solution.py:31
  436.1 3.4 collective-permute-start.4
  439.6 1.9 collective-permute-start.5
  441.5 3.6 collective-permute-done.5
  445.2 3.7 collective-permute-start.6
  448.9 1.3 collective-permute-start.7
  450.2 0.6 collective-permute-done.6
  450.8 3.8 collective-permute-done.7
  455.3 0.9 copy-done.1
  458.7 102.7 %psum.46 = f32[128]{0:T(128)S(1)} all-reduce(f32[128]{0:T(128)S(1)} %get-tuple-element.27), channel_id=1, replica_groups=mesh['gy'=32,'gz'=16] {'gy','gz'}, use_global_device_ids=true, to_apply=%region_9.10 | all-reduce | flops 128 | bytes 1024 | tf_op jit(solution)/shard_map/psum | solution.py:28
  561.5 99.5 %psum.47 = f32[128]{0:T(128)S(1)} all-reduce(f32[128]{0:T(128)S(1)} %multiply_reduce_fusion), channel_id=1, replica_groups=mesh['gy'=32,'gz'=16] {'gy','gz'}, use_global_device_ids=true, to_apply=%region_11.12 | all-reduce | flops 128 | bytes 1024 | tf_op jit(solution)/shard_map/psum | solution.py:31
  661.2 0.8 copy.13
  (54 shorter events, 7.3 us)
Async XLA Ops:
  0.0 1.7 copy-start.4
  0.0 211.4 %copy-start.2 = (f32[3,128]{1,0:T(4,128)S(1)}, f32[3,128]{1,0:T(4,128)}, u32[]{:S(2)}) copy-start(f32[3,128]{1,0:T(4,128)} %param.11) | copy-start | bytes 4612
  0.0 211.4 %copy-start.3 = (f32[3,128]{1,0:T(4,128)S(1)}, f32[3,128]{1,0:T(4,128)}, u32[]{:S(2)}) copy-start(f32[3,128]{1,0:T(4,128)} %param.10) | copy-start | bytes 4612
  211.6 4.8 collective-permute-start
  214.5 5.6 collective-permute-start.1
  220.1 5.6 collective-permute-start.2
  223.8 5.7 collective-permute-start.3
  230.0 1.2 copy-start
  436.1 5.4 collective-permute-start.4
  439.6 5.6 collective-permute-start.5
  445.2 5.6 collective-permute-start.6
  448.9 5.7 collective-permute-start.7
  455.1 1.2 copy-start.1
where the time goes:
time: 663 us; the launch traced here: 662 us
  blocking collectives  614 us (93%)
  starting transfers between devices  20.1 us (3%)
  waiting for transfers between devices  16.1 us (2%)
    psum x3, blocking collectives, moments(): total = lax.psum(jnp.sum(inner, axis=(1, 2, 3)), ('gy', 'gz'))  317 us
    psum x3, blocking collectives, moments(): lax.psum(jnp.sum(centered * centered, axis=(1, 2, 3)), ('gy', 'gz')) / count  297 us
    ppermute x4, waiting for transfers between devices, padded_2(): after = lax.ppermute(leading, axis, down)  14.9 us
    ppermute x4, starting transfers between devices, padded_2(): before = lax.ppermute(last, axis, up)  13.7 us
  transfers between devices with their start and end apart: 8, of which 6 were waited for; matrix products, arithmetic and copies ran while one was open for 0% of the time, Pallas kernels for 0%

commit v1 on v0

v1 whole, which is shorter than its diff:
```python
import jax
import jax.numpy as jnp
from jax import lax
from jax.sharding import Mesh
from jax.sharding import PartitionSpec as P

ROWS = ("x", "y", "core")
DEPTH = "z"


def rim(value, axis, dim):
    count, length = (lax.axis_size(axis), value.shape[dim])
    up = [(i, i + 1) for i in range(count - 1)]
    down = [(j, i) for i, j in up]
    before = lax.ppermute(lax.slice_in_dim(value, length - 1, length, axis=dim), axis, up)
    after = lax.ppermute(lax.slice_in_dim(value, 0, 1, axis=dim), axis, down)
    return before, after


def merged(stats, axis, count):
    parts = lax.axis_size(axis)
    sent = jnp.broadcast_to(stats[None], (parts,) + stats.shape)
    held = lax.all_to_all(sent, axis, 0, 0)
    mean = jnp.mean(held[:, 0], axis=0)
    apart = held[:, 0] - mean
    spread = jnp.sum(held[:, 1] + count * (apart * apart), axis=0)
    return jnp.stack([mean, spread])


def local_moments(inner):
    mean = jnp.mean(inner, axis=(1, 2, 3))
    centered = inner - mean[:, None, None, None]
    return jnp.stack([mean, jnp.sum(centered * centered, axis=(1, 2, 3))])


def moments(inner, with_rim):
    count = float(inner.shape[1] * inner.shape[2] * inner.shape[3])
    stats = local_moments(inner)
    wide = inner
    if with_rim:
        before, after = rim(wide, DEPTH, 2)
    stats = merged(stats, ROWS, count)
    count *= lax.axis_size(ROWS)
    if with_rim:
        wide = jnp.concatenate([before, wide, after], axis=2)
        before, after = rim(wide, ROWS, 1)
    stats = merged(stats, DEPTH, count)
    count *= lax.axis_size(DEPTH)
    if with_rim:
        wide = jnp.concatenate([before, wide, after], axis=1)
    return stats[0], stats[1] / count, wide


def leaky(value):
    return jnp.where(value >= 0.0, value, 0.01 * value)


def normalize(value, mean, spread, gain, shift):
    scaled = (value - mean[:, None, None, None]) / jnp.sqrt(spread + 1e-05)[:, None, None, None]
    return leaky(scaled * gain[:, None, None, None] + shift[:, None, None, None]).astype(jnp.bfloat16)


def inside(axis, length):
    index, count = lax.axis_index(axis), lax.axis_size(axis)
    plane = jnp.arange(length)
    first = (plane > 0) | (index > 0)
    last = (plane < length - 1) | (index < count - 1)
    return first & last


def padded(wide, mean, spread, gain, shift):
    value = normalize(wide, mean, spread, gain, shift)
    keep = inside(ROWS, wide.shape[1])[:, None] & inside(DEPTH, wide.shape[2])[None, :]
    return jnp.where(keep[None, :, :, None], value, jnp.zeros_like(value))


def strided(volume, down_weight):
    blocks = volume.reshape(
        volume.shape[0], volume.shape[1] // 2, 2, volume.shape[2] // 2, 2, volume.shape[3] // 2, 2
    )
    return jnp.einsum(
        "oiabc,iyazbxc->oyzx", down_weight, blocks, preferred_element_type=jnp.float32
    )


def convolve(field, conv_weight):
    rows, depth, length = (field.shape[1] - 2, field.shape[2] - 2, field.shape[3])
    widened = jnp.pad(field, ((0, 0), (0, 0), (0, 0), (1, 1)))
    stacked = jnp.concatenate(
        [widened[:, :, :, offset : offset + length] for offset in range(3)], axis=0
    )
    total = jnp.zeros((conv_weight.shape[2], rows, depth, length), jnp.float32)
    for row_tap in range(3):
        for depth_tap in range(3):
            piece = stacked[:, row_tap : row_tap + rows, depth_tap : depth_tap + depth, :]
            total = total + jnp.einsum(
                "ok,kyzx->oyzx",
                conv_weight[row_tap, depth_tap],
                piece,
                preferred_element_type=jnp.float32,
            )
    return total


def on_device(volume, down_weight, conv_one, conv_two, norm_gain, norm_shift):
    coarse = strided(volume, down_weight)
    mean, spread, wide = moments(coarse, True)
    first = padded(wide, mean, spread, norm_gain[0], norm_shift[0])
    middle = convolve(first, conv_one)
    mean, spread, wide = moments(middle, True)
    second = padded(wide, mean, spread, norm_gain[1], norm_shift[1])
    last = convolve(second, conv_two)
    mean, spread, _ = moments(last, False)
    return normalize(last, mean, spread, norm_gain[2], norm_shift[2])


def solution(mesh):
    split = Mesh(mesh.devices.reshape(4, 4, 2, 16), ROWS + (DEPTH,))
    return jax.shard_map(
        on_device,
        mesh=split,
        in_specs=(P(None, ROWS, DEPTH, None), P(), P(), P(), P(), P()),
        out_specs=P(None, ROWS, DEPTH, None),
        check_vma=False,
    )
```

time: 663 us -> 147 us (0.22)
  blocking collectives: 614 us -> 51.3 us
  starting transfers between devices: 20.1 us -> 46.8 us
  waiting for transfers between devices: 16.1 us -> 33.8 us
    psum x6 -> x0, blocking collectives: 614 us -> none  [the longest x3 317 us: moments(): total = lax.psum(jnp.sum(inner, axis=(1, 2, 3)), ('gy', 'gz'))]
    all_to_all x0 -> x3, blocking collectives: none -> 51.3 us  [merged(): held = lax.all_to_all(sent, axis, 0, 0)]
    all_to_all x0 -> x3, starting transfers between devices: none -> 26.9 us  [merged(): held = lax.all_to_all(sent, axis, 0, 0)]
    all_to_all x0 -> x3, waiting for transfers between devices: none -> 22.3 us  [merged(): held = lax.all_to_all(sent, axis, 0, 0)]
  transfers between devices with their start and end apart: 8 -> 11, of which waited for: 6 -> 7; matrix products, arithmetic and copies ran while one was open for 0% -> 1% of each run, Pallas kernels for 0% -> 0%
where the time goes in v1:
time: 147 us; the launch traced here: 146 us
  blocking collectives  51.3 us (35%)
  starting transfers between devices  46.8 us (32%)
  waiting for transfers between devices  33.8 us (23%)
  local copies, waits for them, and re-layouts  6.9 us (5%)
  matrix products  5.16 us (4%)
  other arithmetic  1.57 us (1%)
    all_to_all x3, blocking collectives, merged(): held = lax.all_to_all(sent, axis, 0, 0)  51.3 us
    all_to_all x3, starting transfers between devices, merged(): held = lax.all_to_all(sent, axis, 0, 0)  26.9 us
    all_to_all x3, waiting for transfers between devices, merged(): held = lax.all_to_all(sent, axis, 0, 0)  22.3 us
    ppermute x4, starting transfers between devices, rim(): lax.ppermute(lax.slice_in_dim(value, length - 1, length, axis=dim), axis,...  13.5 us
    ppermute x4, waiting for transfers between devices, rim(): after = lax.ppermute(lax.slice_in_dim(value, 0, 1, axis=dim), axis, down)  8.8 us
    ppermute x4, starting transfers between devices, rim(): after = lax.ppermute(lax.slice_in_dim(value, 0, 1, axis=dim), axis, down)  6.43 us
    dot_general x18, matrix products, convolve(): jnp.einsum('ok,kyzx->oyzx', conv_weight[row_tap, depth_tap], piece, prefe...  4.78 us
    unnamed x11, local copies, waits for them, and re-layouts  3.37 us
  transfers between devices with their start and end apart: 11, of which 7 were waited for; matrix products, arithmetic and copies ran while one was open for 1% of the time, Pallas kernels for 0%

profile of v1, /device:TPU:1, one launch (start us, length us, event | category | flops | bytes accessed | tf_op | source)
XLA Modules:
  0.0 146.0 jit_solution(14154161429521117456)
XLA Ops:
  0.0 1.7 %copy.28 = bf16[64,4,4,256]{0,3,2,1:T(8,128)(2,1)S(1)} copy(bf16[64,4,4,256]{3,2,1,0:T(4,128)(2,1)} %param.6) | data formatting | bytes 1048576 | tf_op args[0]
  2.8 10.3 %all-to-all-start = ((f32[32,2,128]{2,1,0:T(2,128)}), f32[32,2,128]{2,1,0:T(2,128)S(1)}, u32[]{:S(2)}, u32[]{:S(2)}) async-start(f32[32,2,128]{2,1,0:T(2,128)} %broadcast_in_dim.24), calls=%async_computation | async-start | bytes 65536 | tf_op jit(solution)/shard_map/all_to_all | solution.py:23
  13.2 1.8 %collective-permute-start = (f32[128,2,1,128]{0,3,2,1:T(8,128)S(1)}, f32[128,2,1,128]{0,3,2,1:T(8,128)S(1)}, u32[]{:S(2)}, u32[]{:S(2)}) collective-permute-start(f32[128,2,1,128]{0,3,2,1:T(8,128)S(1)} %get-tuple-element.15), channel_id=1, source_target_pairs={{0,1},{1,2},{2,3},{3,4},{4,5},{5,6},{6,7},{7,8},{8,9},{9,10},{10,1... | collective-permute-start | bytes 393224 | tf_op jit(solution)/shard_map/ppermute | solution.py:15
  15.0 1.3 collective-permute-start.1
  16.4 4.2 %all-to-all-done = f32[32,2,128]{2,1,0:T(2,128)S(1)} async-done(((f32[32,2,128]{2,1,0:T(2,128)}), f32[32,2,128]{2,1,0:T(2,128)S(1)}, u32[]{:S(2)}, u32[]{:S(2)}) %all-to-all-start) | async-done | bytes 32800 | tf_op jit(solution)/shard_map/all_to_all | solution.py:23
  21.3 13.0 %all-to-all-start.1 = ((f32[16,2,128]{2,1,0:T(2,128)}), f32[16,2,128]{2,1,0:T(2,128)S(1)}, u32[]{:S(2)}, u32[]{:S(2)}) async-start(f32[16,2,128]{2,1,0:T(2,128)} %broadcast_in_dim.25), calls=%async_computation.1 | async-start | bytes 32768 | tf_op jit(solution)/shard_map/all_to_all | solution.py:23
  34.4 11.3 %all-to-all-done.1 = f32[16,2,128]{2,1,0:T(2,128)S(1)} async-done(((f32[16,2,128]{2,1,0:T(2,128)}), f32[16,2,128]{2,1,0:T(2,128)S(1)}, u32[]{:S(2)}, u32[]{:S(2)}) %all-to-all-start.1) | async-done | bytes 16416 | tf_op jit(solution)/shard_map/all_to_all | solution.py:23
  45.9 4.8 %collective-permute-start.2 = (f32[128,1,4,128]{0,3,2,1:T(8,128)S(1)}, f32[128,1,4,128]{0,3,2,1:T(8,128)S(1)}, u32[]{:S(2)}, u32[]{:S(2)}) collective-permute-start(f32[128,1,4,128]{0,3,2,1:T(8,128)S(1)} %get-tuple-element.11), channel_id=1, source_target_pairs={{0,16},{16,32},{32,48},{48,64},{64,80},{80,96},{96,112},{112,128},... | collective-permute-start | bytes 786440 | tf_op jit(solution)/shard_map/ppermute | solution.py:15
  50.7 1.9 %collective-permute-start.3 = (f32[128,1,4,128]{0,3,2,1:T(8,128)S(1)}, f32[128,1,4,128]{0,3,2,1:T(8,128)S(1)}, u32[]{:S(2)}, u32[]{:S(2)}) collective-permute-start(f32[128,1,4,128]{0,3,2,1:T(8,128)S(1)} %get-tuple-element.12), channel_id=1, source_target_pairs={{16,0},{32,16},{48,32},{64,48},{80,64},{96,80},{112,96},{128,112},... | collective-permute-start | bytes 786440 | tf_op jit(solution)/shard_map/ppermute | solution.py:16
  52.7 1.3 collective-permute-done.2
  54.0 4.4 %collective-permute-done.3 = f32[128,1,4,128]{0,3,2,1:T(8,128)S(1)} collective-permute-done((f32[128,1,4,128]{0,3,2,1:T(8,128)S(1)}, f32[128,1,4,128]{0,3,2,1:T(8,128)S(1)}, u32[]{:S(2)}, u32[]{:S(2)}) %collective-permute-start.3) | collective-permute-done | bytes 262176 | tf_op jit(solution)/shard_map/ppermute | solution.py:16
  59.1 0.8 copy-done.2
  62.5 15.6 %all_to_all.30 = f32[32,2,128]{2,1,0:T(2,128)S(1)} all-to-all(f32[32,2,128]{2,1,0:T(2,128)S(1)} %broadcast_in_dim.26), channel_id=1, replica_groups=mesh['x'=4,'y'=4,'core'=2,'z'=16] {'x','y','core'}, dimensions={0} | all-to-all | bytes 65536 | tf_op jit(solution)/shard_map/all_to_all | solution.py:23
  78.7 3.5 %all-to-all-start.3 = ((f32[16,2,128]{2,1,0:T(2,128)}), f32[16,2,128]{2,1,0:T(2,128)S(1)}, u32[]{:S(2)}, u32[]{:S(2)}) async-start(f32[16,2,128]{2,1,0:T(2,128)} %broadcast_in_dim.27), calls=%async_computation.3 | async-start | bytes 32768 | tf_op jit(solution)/shard_map/all_to_all | solution.py:23
  82.3 3.2 %collective-permute-start.4 = (f32[128,2,1,128]{0,3,2,1:T(8,128)S(1)}, f32[128,2,1,128]{0,3,2,1:T(8,128)S(1)}, u32[]{:S(2)}, u32[]{:S(2)}) collective-permute-start(f32[128,2,1,128]{0,3,2,1:T(8,128)S(1)} %get-tuple-element.13), channel_id=1, source_target_pairs={{0,1},{1,2},{2,3},{3,4},{4,5},{5,6},{6,7},{7,8},{8,9},{9,10},{10,1... | collective-permute-start | bytes 393224 | tf_op jit(solution)/shard_map/ppermute | solution.py:15
  85.4 1.3 collective-permute-start.5
  86.7 6.8 %all-to-all-done.3 = f32[16,2,128]{2,1,0:T(2,128)S(1)} async-done(((f32[16,2,128]{2,1,0:T(2,128)}), f32[16,2,128]{2,1,0:T(2,128)S(1)}, u32[]{:S(2)}, u32[]{:S(2)}) %all-to-all-start.3) | async-done | bytes 16416 | tf_op jit(solution)/shard_map/all_to_all | solution.py:23
  93.7 3.7 %collective-permute-start.6 = (f32[128,1,4,128]{0,3,2,1:T(8,128)S(1)}, f32[128,1,4,128]{0,3,2,1:T(8,128)S(1)}, u32[]{:S(2)}, u32[]{:S(2)}) collective-permute-start(f32[128,1,4,128]{0,3,2,1:T(8,128)S(1)} %get-tuple-element.7), channel_id=1, source_target_pairs={{0,16},{16,32},{32,48},{48,64},{64,80},{80,96},{96,112},{112,128},... | collective-permute-start | bytes 786440 | tf_op jit(solution)/shard_map/ppermute | solution.py:15
  97.4 1.9 %collective-permute-start.7 = (f32[128,1,4,128]{0,3,2,1:T(8,128)S(1)}, f32[128,1,4,128]{0,3,2,1:T(8,128)S(1)}, u32[]{:S(2)}, u32[]{:S(2)}) collective-permute-start(f32[128,1,4,128]{0,3,2,1:T(8,128)S(1)} %get-tuple-element.8), channel_id=1, source_target_pairs={{16,0},{32,16},{48,32},{64,48},{80,64},{96,80},{112,96},{128,112},... | collective-permute-start | bytes 786440 | tf_op jit(solution)/shard_map/ppermute | solution.py:16
  99.4 1.3 collective-permute-done.6
  100.7 4.4 %collective-permute-done.7 = f32[128,1,4,128]{0,3,2,1:T(8,128)S(1)} collective-permute-done((f32[128,1,4,128]{0,3,2,1:T(8,128)S(1)}, f32[128,1,4,128]{0,3,2,1:T(8,128)S(1)}, u32[]{:S(2)}, u32[]{:S(2)}) %collective-permute-start.7) | collective-permute-done | bytes 262176 | tf_op jit(solution)/shard_map/ppermute | solution.py:16
  105.7 0.8 copy-done.3
  109.2 14.9 %all_to_all.31 = f32[32,2,128]{2,1,0:T(2,128)S(1)} all-to-all(f32[32,2,128]{2,1,0:T(2,128)S(1)} %broadcast_in_dim.28), channel_id=1, replica_groups=mesh['x'=4,'y'=4,'core'=2,'z'=16] {'x','y','core'}, dimensions={0} | all-to-all | bytes 65536 | tf_op jit(solution)/shard_map/all_to_all | solution.py:23
  124.2 20.9 %all_to_all.32 = f32[16,2,128]{2,1,0:T(2,128)S(1)} all-to-all(f32[16,2,128]{2,1,0:T(2,128)S(1)} %broadcast_in_dim.29), channel_id=1, replica_groups=mesh['x'=4,'y'=4,'core'=2,'z'=16] {'z'}, dimensions={0} | all-to-all | bytes 32768 | tf_op jit(solution)/shard_map/all_to_all | solution.py:23
  (91 shorter events, 10.3 us)
Async XLA Ops:
  0.0 1.7 %copy-start.4 = (bf16[128,64,2,2,2]{0,4,3,2,1:T(2,128)(2,1)S(1)}, bf16[128,64,2,2,2]{0,4,3,2,1:T(2,128)(2,1)}, u32[]{:S(2)}) copy-start(bf16[128,64,2,2,2]{0,4,3,2,1:T(2,128)(2,1)} %param.7) | copy-start | bytes 393220
  1.7 14.6 %copy-start = (f32[3,128]{1,0:T(4,128)S(1)}, f32[3,128]{1,0:T(4,128)}, u32[]{:S(2)}) copy-start(f32[3,128]{1,0:T(4,128)} %param.11) | copy-start | bytes 4612
  1.7 14.6 %copy-start.1 = (f32[3,128]{1,0:T(4,128)S(1)}, f32[3,128]{1,0:T(4,128)}, u32[]{:S(2)}) copy-start(f32[3,128]{1,0:T(4,128)} %param.10) | copy-start | bytes 4612
  2.8 17.7 %all-to-all-start = ((f32[32,2,128]{2,1,0:T(2,128)}), f32[32,2,128]{2,1,0:T(2,128)S(1)}, u32[]{:S(2)}, u32[]{:S(2)}) async-start(f32[32,2,128]{2,1,0:T(2,128)} %broadcast_in_dim.24), calls=%async_computation | async-start | bytes 65536 | tf_op jit(solution)/shard_map/all_to_all | solution.py:23
  13.2 32.6 %collective-permute-start = (f32[128,2,1,128]{0,3,2,1:T(8,128)S(1)}, f32[128,2,1,128]{0,3,2,1:T(8,128)S(1)}, u32[]{:S(2)}, u32[]{:S(2)}) collective-permute-start(f32[128,2,1,128]{0,3,2,1:T(8,128)S(1)} %get-tuple-element.15), channel_id=1, source_target_pairs={{0,1},{1,2},{2,3},{3,4},{4,5},{5,6},{6,7},{7,8},{8,9},{9,10},{10,1... | collective-permute-start | bytes 393224 | tf_op jit(solution)/shard_map/ppermute | solution.py:15
  15.0 30.8 %collective-permute-start.1 = (f32[128,2,1,128]{0,3,2,1:T(8,128)S(1)}, f32[128,2,1,128]{0,3,2,1:T(8,128)S(1)}, u32[]{:S(2)}, u32[]{:S(2)}) collective-permute-start(f32[128,2,1,128]{0,3,2,1:T(8,128)S(1)} %get-tuple-element.16), channel_id=1, source_target_pairs={{1,0},{2,1},{3,2},{4,3},{5,4},{6,5},{7,6},{8,7},{9,8},{10,9},{11,1... | collective-permute-start | bytes 393224 | tf_op jit(solution)/shard_map/ppermute | solution.py:16
  21.3 24.4 %all-to-all-start.1 = ((f32[16,2,128]{2,1,0:T(2,128)}), f32[16,2,128]{2,1,0:T(2,128)S(1)}, u32[]{:S(2)}, u32[]{:S(2)}) async-start(f32[16,2,128]{2,1,0:T(2,128)} %broadcast_in_dim.25), calls=%async_computation.1 | async-start | bytes 32768 | tf_op jit(solution)/shard_map/all_to_all | solution.py:23
  45.9 8.1 %collective-permute-start.2 = (f32[128,1,4,128]{0,3,2,1:T(8,128)S(1)}, f32[128,1,4,128]{0,3,2,1:T(8,128)S(1)}, u32[]{:S(2)}, u32[]{:S(2)}) collective-permute-start(f32[128,1,4,128]{0,3,2,1:T(8,128)S(1)} %get-tuple-element.11), channel_id=1, source_target_pairs={{0,16},{16,32},{32,48},{48,64},{64,80},{80,96},{96,112},{112,128},... | collective-permute-start | bytes 786440 | tf_op jit(solution)/shard_map/ppermute | solution.py:15
  50.7 7.7 %collective-permute-start.3 = (f32[128,1,4,128]{0,3,2,1:T(8,128)S(1)}, f32[128,1,4,128]{0,3,2,1:T(8,128)S(1)}, u32[]{:S(2)}, u32[]{:S(2)}) collective-permute-start(f32[128,1,4,128]{0,3,2,1:T(8,128)S(1)} %get-tuple-element.12), channel_id=1, source_target_pairs={{16,0},{32,16},{48,32},{64,48},{80,64},{96,80},{112,96},{128,112},... | collective-permute-start | bytes 786440 | tf_op jit(solution)/shard_map/ppermute | solution.py:16
  58.7 1.2 copy-start.2
  78.7 14.8 %all-to-all-start.3 = ((f32[16,2,128]{2,1,0:T(2,128)}), f32[16,2,128]{2,1,0:T(2,128)S(1)}, u32[]{:S(2)}, u32[]{:S(2)}) async-start(f32[16,2,128]{2,1,0:T(2,128)} %broadcast_in_dim.27), calls=%async_computation.3 | async-start | bytes 32768 | tf_op jit(solution)/shard_map/all_to_all | solution.py:23
  82.3 11.3 %collective-permute-start.4 = (f32[128,2,1,128]{0,3,2,1:T(8,128)S(1)}, f32[128,2,1,128]{0,3,2,1:T(8,128)S(1)}, u32[]{:S(2)}, u32[]{:S(2)}) collective-permute-start(f32[128,2,1,128]{0,3,2,1:T(8,128)S(1)} %get-tuple-element.13), channel_id=1, source_target_pairs={{0,1},{1,2},{2,3},{3,4},{4,5},{5,6},{6,7},{7,8},{8,9},{9,10},{10,1... | collective-permute-start | bytes 393224 | tf_op jit(solution)/shard_map/ppermute | solution.py:15
  85.4 8.2 %collective-permute-start.5 = (f32[128,2,1,128]{0,3,2,1:T(8,128)S(1)}, f32[128,2,1,128]{0,3,2,1:T(8,128)S(1)}, u32[]{:S(2)}, u32[]{:S(2)}) collective-permute-start(f32[128,2,1,128]{0,3,2,1:T(8,128)S(1)} %get-tuple-element.14), channel_id=1, source_target_pairs={{1,0},{2,1},{3,2},{4,3},{5,4},{6,5},{7,6},{8,7},{9,8},{10,9},{11,1... | collective-permute-start | bytes 393224 | tf_op jit(solution)/shard_map/ppermute | solution.py:16
  93.7 7.0 %collective-permute-start.6 = (f32[128,1,4,128]{0,3,2,1:T(8,128)S(1)}, f32[128,1,4,128]{0,3,2,1:T(8,128)S(1)}, u32[]{:S(2)}, u32[]{:S(2)}) collective-permute-start(f32[128,1,4,128]{0,3,2,1:T(8,128)S(1)} %get-tuple-element.7), channel_id=1, source_target_pairs={{0,16},{16,32},{32,48},{48,64},{64,80},{80,96},{96,112},{112,128},... | collective-permute-start | bytes 786440 | tf_op jit(solution)/shard_map/ppermute | solution.py:15
  97.4 7.7 %collective-permute-start.7 = (f32[128,1,4,128]{0,3,2,1:T(8,128)S(1)}, f32[128,1,4,128]{0,3,2,1:T(8,128)S(1)}, u32[]{:S(2)}, u32[]{:S(2)}) collective-permute-start(f32[128,1,4,128]{0,3,2,1:T(8,128)S(1)} %get-tuple-element.8), channel_id=1, source_target_pairs={{16,0},{32,16},{48,32},{64,48},{80,64},{96,80},{112,96},{128,112},... | collective-permute-start | bytes 786440 | tf_op jit(solution)/shard_map/ppermute | solution.py:16
  105.4 1.2 copy-start.3

commit v2 on v1

v2 whole, which is shorter than its diff:
```python
import functools

import jax
import jax.numpy as jnp
from jax import lax
from jax.experimental import pallas as pl
from jax.experimental.pallas import tpu as pltpu
from jax.sharding import Mesh
from jax.sharding import PartitionSpec as P


ROWS = ("x", "y", "core")
DEPTH = "z"


def neighbours(value, axis):
    count = lax.axis_size(axis)
    up = [(i, i + 1) for i in range(count - 1)]
    down = [(j, i) for i, j in up]
    before = lax.ppermute(value, axis, up)
    after = lax.ppermute(value, axis, down)
    return before, after


def pooled(stats, axis, count):
    parts = lax.axis_size(axis)
    sent = jnp.broadcast_to(stats[None], (parts,) + stats.shape)
    held = lax.all_to_all(sent, axis, 0, 0)
    mean = jnp.mean(held[:, 0], axis=0)
    apart = held[:, 0] - mean
    spread = jnp.sum(held[:, 1] + count * (apart * apart), axis=0)
    return jnp.stack([mean, spread])


def affine(stats, count, gain, shift):
    scale = gain / jnp.sqrt(stats[1] / count + 1e-05)
    return jnp.stack([stats[0], scale, shift])


def inside(axis, own, rim):
    plane = lax.axis_index(axis) * own - rim + jnp.arange(own + 2 * rim)
    return ((plane >= 0) & (plane < own * lax.axis_size(axis))).astype(jnp.float32)


def leaky(value):
    return jnp.where(value >= 0.0, value, 0.01 * value)


def conv_kernel(pieces, rows, depth, rim, keep, norm, *refs):
    fields, (source, out, stats, stacked, weight, arrived) = refs[:pieces], refs[pieces:]
    fetches = [
        pltpu.make_async_copy(source.at[tap], weight.at[tap], arrived.at[tap]) for tap in range(3)
    ]
    for fetch in fetches:
        fetch.start()
    length, channels = fields[0].shape[2:]
    each = rows // pieces
    mean, scale, shift = norm[0:1, :], norm[1:2, :], norm[2:3, :]
    place = lax.broadcasted_iota(jnp.int32, (length, channels), 0)

    for piece, field in enumerate(fields):
        @pl.loop(0, each * depth)
        def _(index, piece=piece, field=field):
            row, cell = index // depth, index % depth
            value = (field[row, cell] - mean) * scale + shift
            value = leaky(value) * keep[piece * each * depth + index]
            left = jnp.where(place > 0, pltpu.roll(value, 1, 0), 0.0)
            right = jnp.where(place < length - 1, pltpu.roll(value, length - 1, 0), 0.0)
            at = piece * each * depth + index
            stacked[at, :, 0:channels] = left.astype(jnp.bfloat16)
            stacked[at, :, channels : 2 * channels] = value.astype(jnp.bfloat16)
            stacked[at, :, 2 * channels :] = right.astype(jnp.bfloat16)

    cells = depth - 2
    for fetch in fetches:
        fetch.wait()

    def row_of(row):
        total = jnp.zeros((cells * length, channels), jnp.float32)
        for row_tap in range(3):
            for depth_tap in range(3):
                start = (row + row_tap) * depth + depth_tap
                piece = stacked[pl.ds(start, cells)].reshape(cells * length, 3 * channels)
                total = total + lax.dot_general(
                    piece,
                    weight[row_tap, depth_tap],
                    (((1,), (1,)), ((), ())),
                    preferred_element_type=jnp.float32,
                )
        out[row] = total.reshape(cells, length, channels)

    for row in range(rows - 2):
        row_of(row)

    inner = [
        out[row, cell]
        for row in range(rim, rows - 2 - rim)
        for cell in range(rim, cells - rim)
    ]
    middle = sum(jnp.sum(plane, axis=0, keepdims=True) for plane in inner) / (len(inner) * length)
    apart = [plane - middle for plane in inner]
    spread = sum(jnp.sum(plane * plane, axis=0, keepdims=True) for plane in apart)
    stats[0:1, :] = middle
    stats[1:2, :] = spread


def convolve(fields, weight, keep, norm, rim):
    pieces = len(fields)
    rows = pieces * fields[0].shape[0]
    depth, length, channels = fields[0].shape[1:]
    in_vmem = pl.BlockSpec(memory_space=pltpu.VMEM)
    flops = 2 * (rows - 2) * (depth - 2) * length * channels * channels * 27
    return pl.pallas_call(
        functools.partial(conv_kernel, pieces, rows, depth, rim),
        out_shape=(
            jax.ShapeDtypeStruct((rows - 2, depth - 2, length, channels), jnp.float32),
            jax.ShapeDtypeStruct((2, channels), jnp.float32),
        ),
        in_specs=[pl.BlockSpec(memory_space=pltpu.SMEM), in_vmem] + [in_vmem] * pieces
        + [pl.BlockSpec(memory_space=pltpu.HBM)],
        out_specs=(in_vmem, in_vmem),
        scratch_shapes=[
            pltpu.VMEM((rows * depth, length, 3 * channels), jnp.bfloat16),
            pltpu.VMEM(weight.shape, weight.dtype),
            pltpu.SemaphoreType.DMA((3,)),
        ],
        compiler_params=pltpu.CompilerParams(vmem_limit_bytes=16 << 20),
        cost_estimate=pl.CostEstimate(flops=flops, bytes_accessed=2 << 20, transcendentals=0),
    )(keep.reshape(-1), norm, *fields, pltpu.with_memory_space_constraint(weight, pltpu.HBM))


def strided(volume, down_weight):
    blocks = volume.reshape(
        volume.shape[0], volume.shape[1] // 2, 2, volume.shape[2] // 2, 2, volume.shape[3] // 2, 2
    )
    return jnp.einsum(
        "oiabc,iyazbxc->yzxo", down_weight, blocks, preferred_element_type=jnp.float32
    )


def local_moments(inner):
    mean = jnp.mean(inner, axis=(0, 1, 2))
    centered = inner - mean
    return jnp.stack([mean, jnp.sum(centered * centered, axis=(0, 1, 2))])


def on_device(volume, down_weight, conv_one, conv_two, norm_gain, norm_shift):
    coarse = strided(volume, down_weight)
    rows, depth, length = coarse.shape[:3]
    own = float(rows * depth * length)
    plane = own * lax.axis_size(ROWS)
    count = plane * lax.axis_size(DEPTH)
    wide_keep = inside(ROWS, rows, 2)[:, None] * inside(DEPTH, depth, 2)[None, :]
    keep = wide_keep[1:-1, 1:-1]

    before, after = neighbours(coarse, DEPTH)
    stats = pooled(local_moments(coarse), ROWS, own)
    wide = jnp.concatenate([before, coarse, after], axis=1)
    before, after = neighbours(wide, ROWS)
    stats = pooled(stats, DEPTH, plane)
    norm = affine(stats, count, norm_gain[0], norm_shift[0])
    middle, stats = convolve([before, wide, after], conv_one, wide_keep, norm, 1)
    stats = pooled(pooled(stats, ROWS, own), DEPTH, plane)
    norm = affine(stats, count, norm_gain[1], norm_shift[1])
    last, stats = convolve([middle], conv_two, keep, norm, 0)
    stats = pooled(pooled(stats, ROWS, own), DEPTH, plane)
    mean, scale, shift = affine(stats, count, norm_gain[2], norm_shift[2])
    features = leaky((last - mean) * scale + shift).astype(jnp.bfloat16)
    return jnp.transpose(features, (3, 0, 1, 2))


def solution(mesh):
    split = Mesh(mesh.devices.reshape(4, 4, 2, 16), ROWS + (DEPTH,))
    return jax.shard_map(
        on_device,
        mesh=split,
        in_specs=(P(None, ROWS, DEPTH, None), P(), P(), P(), P(), P()),
        out_specs=P(None, ROWS, DEPTH, None),
        check_vma=False,
    )
```

time: 147 us -> 130 us (0.88)
  blocking collectives: 51.3 us -> 40.8 us
  Pallas kernels: 0 us -> 8.92 us
  waiting for transfers between devices: 33.8 us -> 26 us
  matrix products: 5.16 us -> 0.37 us
    all_to_all x3, blocking collectives: 51.3 us -> 40.8 us  [pooled(): held = lax.all_to_all(sent, axis, 0, 0)]
    ppermute x8 -> x4, waiting for transfers between devices: 11.5 us -> 2.41 us  [the longest x2 1.23 us: neighbours(): after = lax.ppermute(value, axis, down)]
    pallas_call x0 -> x2, Pallas kernels: none -> 8.92 us  [convolve(): pl.pallas_call(functools.partial(conv_kernel, pieces, rows, depth, rim),...]
    ppermute x8 -> x4, starting transfers between devices: 19.9 us -> 11.9 us  [the longest x2 7.98 us: neighbours(): before = lax.ppermute(value, axis, up)]
    all_to_all x3, starting transfers between devices: 26.9 us -> 34.4 us  [pooled(): held = lax.all_to_all(sent, axis, 0, 0)]
    dot_general x19 -> x1, matrix products: 5.16 us -> 0.37 us  [strided(): jnp.einsum('oiabc,iyazbxc->yzxo', down_weight, blocks, preferred_element_...]
    unnamed x11 -> x7, local copies, waits for them, and re-layouts: 3.37 us -> 2.91 us
  transfers between devices with their start and end apart: 11 -> 7, of which waited for: 7 -> 5; matrix products, arithmetic and copies ran while one was open for 1% -> 2% of each run, Pallas kernels for 0% -> 0%
where the time goes in v2:
time: 130 us
  starting transfers between devices  46.3 us (36%)
  blocking collectives  40.8 us (31%)
  waiting for transfers between devices  26 us (20%)
  Pallas kernels  8.92 us (7%)
  local copies, waits for them, and re-layouts  5.95 us (5%)
  other arithmetic  1.37 us (1%)
    all_to_all x3, blocking collectives, pooled(): held = lax.all_to_all(sent, axis, 0, 0)  40.8 us
    all_to_all x3, starting transfers between devices, pooled(): held = lax.all_to_all(sent, axis, 0, 0)  34.4 us
    all_to_all x3, waiting for transfers between devices, pooled(): held = lax.all_to_all(sent, axis, 0, 0)  23.6 us
    pallas_call x2, Pallas kernels, convolve(): pl.pallas_call(functools.partial(conv_kernel, pieces, rows, depth, rim),...  8.92 us
    ppermute x2, starting transfers between devices, neighbours(): before = lax.ppermute(value, axis, up)  7.98 us
    ppermute x2, starting transfers between devices, neighbours(): after = lax.ppermute(value, axis, down)  3.87 us
    unnamed x7, local copies, waits for them, and re-layouts  2.91 us
  transfers between devices with their start and end apart: 7, of which 5 were waited for; matrix products, arithmetic and copies ran while one was open for 2% of the time, Pallas kernels for 0%

profile of v2, /device:TPU:1, one launch (start us, length us, event | category | flops | bytes accessed | tf_op | source)
XLA Modules:
  0.0 129.8 jit_solution(16460913926914216520)
XLA Ops:
  0.0 1.7 %copy.28 = bf16[64,4,4,256]{0,3,2,1:T(8,128)(2,1)S(1)} copy(bf16[64,4,4,256]{3,2,1,0:T(4,128)(2,1)} %param.6) | data formatting | bytes 1048576 | tf_op args[0]
  2.0 1.3 collective-permute-start.1
  3.3 5.0 %collective-permute-start = (f32[2,2,128,128]{3,2,1,0:T(8,128)S(1)}, f32[2,2,128,128]{3,2,1,0:T(8,128)S(1)}, u32[]{:S(2)}, u32[]{:S(2)}) collective-permute-start(f32[2,2,128,128]{3,2,1,0:T(8,128)S(1)} %get-tuple-element.41), channel_id=1, source_target_pairs={{0,1},{1,2},{2,3},{3,4},{4,5},{5,6},{6,7},{7,8},{8,9},{9,10},{10,1... | collective-permute-start | bytes 786440 | tf_op jit(solution)/shard_map/ppermute | solution.py:20
  8.5 0.6 broadcast_in_dim.12
  9.1 9.9 %all-to-all-start = ((f32[32,2,128]{2,1,0:T(2,128)}), f32[32,2,128]{2,1,0:T(2,128)S(1)}, u32[]{:S(2)}, u32[]{:S(2)}) async-start(f32[32,2,128]{2,1,0:T(2,128)} %broadcast_in_dim.12), calls=%async_computation | async-start | bytes 65536 | tf_op jit(solution)/shard_map/all_to_all | solution.py:28
  19.8 6.6 %all-to-all-done = f32[32,2,128]{2,1,0:T(2,128)S(1)} async-done(((f32[32,2,128]{2,1,0:T(2,128)}), f32[32,2,128]{2,1,0:T(2,128)S(1)}, u32[]{:S(2)}, u32[]{:S(2)}) %all-to-all-start) | async-done | bytes 32800 | tf_op jit(solution)/shard_map/all_to_all | solution.py:28
  26.5 0.6 broadcast_in_dim.13
  27.1 13.0 %all-to-all-start.1 = ((f32[16,2,128]{2,1,0:T(2,128)}), f32[16,2,128]{2,1,0:T(2,128)S(1)}, u32[]{:S(2)}, u32[]{:S(2)}) async-start(f32[16,2,128]{2,1,0:T(2,128)} %broadcast_in_dim.13), calls=%async_computation.1 | async-start | bytes 32768 | tf_op jit(solution)/shard_map/all_to_all | solution.py:28
  40.2 2.6 %collective-permute-start.3 = (f32[2,6,128,128]{3,2,1,0:T(8,128)S(1)}, f32[2,6,128,128]{3,2,1,0:T(8,128)S(1)}, u32[]{:S(2)}, u32[]{:S(2)}) collective-permute-start(f32[2,6,128,128]{3,2,1,0:T(8,128)S(1)} %pad_maximum_fusion.refs_1_), channel_id=1, source_target_pairs={{16,0},{32,16},{48,32},{64,48},{80,64},{96,80},{112,96},{128,112},... | collective-permute-start | bytes 2359304 | tf_op jit(solution)/shard_map/ppermute | solution.py:21
  42.8 3.0 %collective-permute-start.2 = (f32[2,6,128,128]{3,2,1,0:T(8,128)S(1)}, f32[2,6,128,128]{3,2,1,0:T(8,128)S(1)}, u32[]{:S(2)}, u32[]{:S(2)}) collective-permute-start(f32[2,6,128,128]{3,2,1,0:T(8,128)S(1)} %pad_maximum_fusion.refs_1_), channel_id=1, source_target_pairs={{0,16},{16,32},{32,48},{48,64},{64,80},{80,96},{96,112},{112,128},... | collective-permute-start | bytes 2359304 | tf_op jit(solution)/shard_map/ppermute | solution.py:20
  45.8 5.7 %all-to-all-done.1 = f32[16,2,128]{2,1,0:T(2,128)S(1)} async-done(((f32[16,2,128]{2,1,0:T(2,128)}), f32[16,2,128]{2,1,0:T(2,128)S(1)}, u32[]{:S(2)}, u32[]{:S(2)}) %all-to-all-start.1) | async-done | bytes 16416 | tf_op jit(solution)/shard_map/all_to_all | solution.py:28
  51.6 0.7 bitcast_multiply_fusion.2
  52.3 1.2 collective-permute-done.3.refs_2_
  53.5 1.2 collective-permute-done.2.refs_0_
  54.7 6.1 %shard_map.64 = (f32[4,4,128,128]{3,2,1,0:T(8,128)S(1)}, f32[2,128]{1,0:T(2,128)S(1)}) custom-call(f32[36]{0:T(128)S(1)} %mul.89.keep, f32[3,128]{1,0:T(4,128)S(1)} %pad_maximum_fusion.1.norm, f32[2,6,128,128]{3,2,1,0:T(8,128)S(1)} %collective-permute-done.2.refs_0_, f32[2,6,128,128]{3,2,1,0:T(8,128)S(1)} %pad_maximum_fusion.refs_1_, ...), custom_call_target="tpu_custom_call" | custom-call | flops 1811939328 | bytes 2097152 | tf_op jit(solution)/shard_map/pallas_call | solution.py:113
  60.8 14.7 %all_to_all.30 = f32[32,2,128]{2,1,0:T(2,128)S(1)} all-to-all(f32[32,2,128]{2,1,0:T(2,128)S(1)} %broadcast_in_dim.14), channel_id=1, replica_groups=mesh['x'=4,'y'=4,'core'=2,'z'=16] {'x','y','core'}, dimensions={0} | all-to-all | bytes 65536 | tf_op jit(solution)/shard_map/all_to_all | solution.py:28
  75.7 0.6 broadcast_in_dim.15
  76.3 11.5 %all-to-all-start.3 = ((f32[16,2,128]{2,1,0:T(2,128)}), f32[16,2,128]{2,1,0:T(2,128)S(1)}, u32[]{:S(2)}, u32[]{:S(2)}) async-start(f32[16,2,128]{2,1,0:T(2,128)} %broadcast_in_dim.15), calls=%async_computation.3 | async-start | bytes 32768 | tf_op jit(solution)/shard_map/all_to_all | solution.py:28
  87.9 11.2 %all-to-all-done.3 = f32[16,2,128]{2,1,0:T(2,128)S(1)} async-done(((f32[16,2,128]{2,1,0:T(2,128)}), f32[16,2,128]{2,1,0:T(2,128)S(1)}, u32[]{:S(2)}, u32[]{:S(2)}) %all-to-all-start.3) | async-done | bytes 16416 | tf_op jit(solution)/shard_map/all_to_all | solution.py:28
  99.2 0.6 copy-done.2
  99.9 2.8 %shard_map.65 = (f32[2,2,128,128]{3,2,1,0:T(8,128)S(1)}, f32[2,128]{1,0:T(2,128)S(1)}) custom-call(f32[16]{0:T(128)S(1)} %reshape.142.keep, f32[3,128]{1,0:T(4,128)S(1)} %pad_maximum_fusion.2.norm, f32[4,4,128,128]{3,2,1,0:T(8,128)S(1)} %get-tuple-element.10.refs_0_, bf16[3,3,128,384]{3,2,1,0:T(8,128)(2,1)} %refs_1_.1), custom_call_target="tpu_custom_call" | custom-call | flops 452984832 | bytes 2097152 | tf_op jit(solution)/shard_map/pallas_call | solution.py:113
  102.8 12.2 %all_to_all.31 = f32[32,2,128]{2,1,0:T(2,128)S(1)} all-to-all(f32[32,2,128]{2,1,0:T(2,128)S(1)} %broadcast_in_dim.16), channel_id=1, replica_groups=mesh['x'=4,'y'=4,'core'=2,'z'=16] {'x','y','core'}, dimensions={0} | all-to-all | bytes 65536 | tf_op jit(solution)/shard_map/all_to_all | solution.py:28
  115.0 13.9 %all_to_all.32 = f32[16,2,128]{2,1,0:T(2,128)S(1)} all-to-all(f32[16,2,128]{2,1,0:T(2,128)S(1)} %broadcast_in_dim.17), channel_id=1, replica_groups=mesh['x'=4,'y'=4,'core'=2,'z'=16] {'z'}, dimensions={0} | all-to-all | bytes 32768 | tf_op jit(solution)/shard_map/all_to_all | solution.py:28
  129.1 0.8 copy.41
  (53 shorter events, 2.1 us)
Async XLA Ops:
  0.0 1.7 %copy-start = (bf16[128,64,2,2,2]{0,4,3,2,1:T(2,128)(2,1)S(1)}, bf16[128,64,2,2,2]{0,4,3,2,1:T(2,128)(2,1)}, u32[]{:S(2)}) copy-start(bf16[128,64,2,2,2]{0,4,3,2,1:T(2,128)(2,1)} %param.7) | copy-start | bytes 393220
  2.0 38.1 %collective-permute-start.1 = (f32[2,2,128,128]{3,2,1,0:T(8,128)S(1)}, f32[2,2,128,128]{3,2,1,0:T(8,128)S(1)}, u32[]{:S(2)}, u32[]{:S(2)}) collective-permute-start(f32[2,2,128,128]{3,2,1,0:T(8,128)S(1)} %get-tuple-element.41), channel_id=1, source_target_pairs={{1,0},{2,1},{3,2},{4,3},{5,4},{6,5},{7,6},{8,7},{9,8},{10,9},{11,1... | collective-permute-start | bytes 786440 | tf_op jit(solution)/shard_map/ppermute | solution.py:21
  3.3 36.8 %collective-permute-start = (f32[2,2,128,128]{3,2,1,0:T(8,128)S(1)}, f32[2,2,128,128]{3,2,1,0:T(8,128)S(1)}, u32[]{:S(2)}, u32[]{:S(2)}) collective-permute-start(f32[2,2,128,128]{3,2,1,0:T(8,128)S(1)} %get-tuple-element.41), channel_id=1, source_target_pairs={{0,1},{1,2},{2,3},{3,4},{4,5},{5,6},{6,7},{7,8},{8,9},{9,10},{10,1... | collective-permute-start | bytes 786440 | tf_op jit(solution)/shard_map/ppermute | solution.py:20
  9.1 17.3 %all-to-all-start = ((f32[32,2,128]{2,1,0:T(2,128)}), f32[32,2,128]{2,1,0:T(2,128)S(1)}, u32[]{:S(2)}, u32[]{:S(2)}) async-start(f32[32,2,128]{2,1,0:T(2,128)} %broadcast_in_dim.12), calls=%async_computation | async-start | bytes 65536 | tf_op jit(solution)/shard_map/all_to_all | solution.py:28
  19.0 0.7 copy-start.1
  27.1 24.4 %all-to-all-start.1 = ((f32[16,2,128]{2,1,0:T(2,128)}), f32[16,2,128]{2,1,0:T(2,128)S(1)}, u32[]{:S(2)}, u32[]{:S(2)}) async-start(f32[16,2,128]{2,1,0:T(2,128)} %broadcast_in_dim.13), calls=%async_computation.1 | async-start | bytes 32768 | tf_op jit(solution)/shard_map/all_to_all | solution.py:28
  40.2 13.3 %collective-permute-start.3 = (f32[2,6,128,128]{3,2,1,0:T(8,128)S(1)}, f32[2,6,128,128]{3,2,1,0:T(8,128)S(1)}, u32[]{:S(2)}, u32[]{:S(2)}) collective-permute-start(f32[2,6,128,128]{3,2,1,0:T(8,128)S(1)} %pad_maximum_fusion.refs_1_), channel_id=1, source_target_pairs={{16,0},{32,16},{48,32},{64,48},{80,64},{96,80},{112,96},{128,112},... | collective-permute-start | bytes 2359304 | tf_op jit(solution)/shard_map/ppermute | solution.py:21
  42.8 11.9 %collective-permute-start.2 = (f32[2,6,128,128]{3,2,1,0:T(8,128)S(1)}, f32[2,6,128,128]{3,2,1,0:T(8,128)S(1)}, u32[]{:S(2)}, u32[]{:S(2)}) collective-permute-start(f32[2,6,128,128]{3,2,1,0:T(8,128)S(1)} %pad_maximum_fusion.refs_1_), channel_id=1, source_target_pairs={{0,16},{16,32},{32,48},{48,64},{64,80},{80,96},{96,112},{112,128},... | collective-permute-start | bytes 2359304 | tf_op jit(solution)/shard_map/ppermute | solution.py:20
  76.3 22.9 %all-to-all-start.3 = ((f32[16,2,128]{2,1,0:T(2,128)}), f32[16,2,128]{2,1,0:T(2,128)S(1)}, u32[]{:S(2)}, u32[]{:S(2)}) async-start(f32[16,2,128]{2,1,0:T(2,128)} %broadcast_in_dim.15), calls=%async_computation.3 | async-start | bytes 32768 | tf_op jit(solution)/shard_map/all_to_all | solution.py:28
  99.2 0.7 copy-start.2

commit v3 on v2

v3 whole, which is shorter than its diff:
```python
import functools

import jax
import jax.numpy as jnp
from jax import lax
from jax.experimental import pallas as pl
from jax.experimental.pallas import tpu as pltpu
from jax.sharding import Mesh
from jax.sharding import PartitionSpec as P


ROWS = ("x", "y", "core")
DEPTH = "z"


def swaps(value, axis):
    count = lax.axis_size(axis)
    even = [(i, i + 1) for i in range(0, count - 1, 2)]
    odd = [(i, i + 1) for i in range(1, count - 1, 2)]
    got = []
    for pairs in (even, odd):
        got.append(lax.ppermute(value, axis, pairs + [(j, i) for i, j in pairs]))
    return got


def exchanged(stats, axis):
    sent = jnp.broadcast_to(stats[None], (lax.axis_size(axis),) + stats.shape)
    return lax.all_to_all(sent, axis, 0, 0)


def pooled(held, count):
    mean = jnp.mean(held[:, 0], axis=0)
    apart = held[:, 0] - mean
    spread = jnp.sum(held[:, 1] + count * (apart * apart), axis=0)
    return jnp.stack([mean, spread])


def affine(held, count, gain, shift):
    parts = held.shape[0]
    means = [held[part, 0:1, :] for part in range(parts)]
    mean = sum(means) / parts
    spread = sum(
        held[part, 1:2, :] + count * ((means[part] - mean) * (means[part] - mean))
        for part in range(parts)
    )
    return mean, gain / jnp.sqrt(spread / (count * parts) + 1e-05), shift


def leaky(value):
    return jnp.where(value >= 0.0, value, 0.01 * value)


def orders(at, own, swapped):
    if not swapped:
        return [(0, 0, own)]
    odd = lax.rem(at, 2)
    return [(0, own, own), (own, (1 - odd) * 2 * own, own), (2 * own, odd * 2 * own, own)]


def conv_kernel(norm, count, block, whole, rim, swapped, at, held, gains, *refs):
    pieces = 3 if swapped else 1
    fields, (source, out, stats, stacked, weight, arrived) = refs[:pieces], refs[pieces:]
    length, channels = fields[0].shape[2:]
    rows, depth = pieces * fields[0].shape[0], fields[0].shape[1]
    wide = 3 * channels
    fetches = [
        pltpu.make_async_copy(
            source.at[row_tap, depth_tap],
            weight.at[pl.ds(row_tap * channels, channels), pl.ds(depth_tap * wide, wide)],
            arrived.at[row_tap, depth_tap],
        )
        for row_tap in range(3)
        for depth_tap in range(3)
    ]
    for fetch in fetches:
        fetch.start()

    mean, scale, shift = affine(held, count, gains[0, norm : norm + 1, :], gains[1, norm : norm + 1, :])
    place = lax.broadcasted_iota(jnp.int32, (length, channels), 0)
    row_at = at[0] * block[0] - (rows - block[0]) // 2
    depth_at = at[1] * block[1] - (depth - block[1]) // 2
    row_groups = orders(at[0], block[0] if swapped else rows, swapped)
    depth_groups = orders(at[1], block[1] if swapped else depth, swapped)
    for piece, (_, to_row, row_count) in enumerate(row_groups):
        for from_cell, to_cell, cell_count in depth_groups:
            for i in range(row_count):
                for j in range(cell_count):
                    row, cell = to_row + i, to_cell + j
                    y, z = row_at + row, depth_at + cell
                    here = (y >= 0) & (y < whole[0]) & (z >= 0) & (z < whole[1])
                    value = (fields[piece][i, from_cell + j] - mean) * scale + shift
                    value = jnp.maximum(value, 0.01 * value) * jnp.where(here, 1.0, 0.0)
                    left = jnp.where(place > 0, pltpu.roll(value, 1, 0), 0.0)
                    right = jnp.where(place < length - 1, pltpu.roll(value, length - 1, 0), 0.0)
                    slot = row * depth + cell
                    stacked[slot, :, 0:channels] = left.astype(jnp.bfloat16)
                    stacked[slot, :, channels : 2 * channels] = value.astype(jnp.bfloat16)
                    stacked[slot, :, 2 * channels :] = right.astype(jnp.bfloat16)

    for fetch in fetches:
        fetch.wait()

    cells = depth - 2
    for row in range(rows):
        taken = jnp.concatenate(
            [
                stacked[pl.ds(row * depth + depth_tap, cells)].reshape(cells * length, wide)
                for depth_tap in range(3)
            ],
            axis=1,
        )
        taps = [tap for tap in range(3) if 0 <= row - tap < rows - 2]
        product = lax.dot_general(
            taken,
            weight[pl.ds(taps[0] * channels, len(taps) * channels), :],
            (((1,), (1,)), ((), ())),
            preferred_element_type=jnp.float32,
        )
        for place_of, tap in enumerate(taps):
            part = product[:, place_of * channels : (place_of + 1) * channels]
            part = part.reshape(cells, length, channels)
            if tap == 0:
                out[row] = part
            else:
                out[row - tap] += part

    inner = [
        out[row, cell]
        for row in range(rim, rows - 2 - rim)
        for cell in range(rim, cells - rim)
    ]
    middle = sum(jnp.sum(plane, axis=0, keepdims=True) for plane in inner) / (len(inner) * length)
    apart = [plane - middle for plane in inner]
    spread = sum(jnp.sum(plane * plane, axis=0, keepdims=True) for plane in apart)
    stats[0:1, :] = middle
    stats[1:2, :] = spread


def convolve(norm, count, block, whole, rim, at, held, gains, fields, weight):
    pieces = len(fields)
    rows = pieces * fields[0].shape[0]
    depth, length, channels = fields[0].shape[1:]
    in_vmem = pl.BlockSpec(memory_space=pltpu.VMEM)
    flops = 2 * (rows - 2) * (depth - 2) * length * channels * channels * 27
    return pl.pallas_call(
        functools.partial(conv_kernel, norm, count, block, whole, rim, pieces == 3),
        out_shape=(
            jax.ShapeDtypeStruct((rows - 2, depth - 2, length, channels), jnp.float32),
            jax.ShapeDtypeStruct((2, channels), jnp.float32),
        ),
        in_specs=[pl.BlockSpec(memory_space=pltpu.SMEM)]
        + [in_vmem] * (2 + pieces)
        + [pl.BlockSpec(memory_space=pltpu.HBM)],
        out_specs=(in_vmem, in_vmem),
        scratch_shapes=[
            pltpu.VMEM((rows * depth, length, 3 * channels), jnp.bfloat16),
            pltpu.VMEM((3 * channels, 9 * channels), weight.dtype),
            pltpu.SemaphoreType.DMA((3, 3)),
        ],
        compiler_params=pltpu.CompilerParams(vmem_limit_bytes=16 << 20),
        cost_estimate=pl.CostEstimate(flops=flops, bytes_accessed=2 << 20, transcendentals=0),
    )(at, held, gains, *fields, pltpu.with_memory_space_constraint(weight, pltpu.HBM))


def strided(volume, down_weight):
    blocks = volume.reshape(
        volume.shape[0], volume.shape[1] // 2, 2, volume.shape[2] // 2, 2, volume.shape[3] // 2, 2
    )
    return jnp.einsum(
        "oiabc,iyazbxc->yzxo", down_weight, blocks, preferred_element_type=jnp.float32
    )


def local_moments(inner):
    mean = jnp.mean(inner, axis=(0, 1, 2))
    centered = inner - mean
    return jnp.stack([mean, jnp.sum(centered * centered, axis=(0, 1, 2))])


def on_device(volume, down_weight, conv_one, conv_two, norm_gain, norm_shift):
    coarse = strided(volume, down_weight)
    rows, depth, length = coarse.shape[:3]
    block = (rows, depth)
    whole = (rows * lax.axis_size(ROWS), depth * lax.axis_size(DEPTH))
    own = float(rows * depth * length)
    plane = own * lax.axis_size(ROWS)
    at = jnp.stack([lax.axis_index(ROWS), lax.axis_index(DEPTH)])
    gains = jnp.stack([norm_gain, norm_shift])

    stats, at, gains, gain, shift = lax.optimization_barrier(
        (local_moments(coarse), at, gains, norm_gain[2], norm_shift[2])
    )
    beside = swaps(coarse, DEPTH)
    stats = pooled(exchanged(stats, ROWS), own)
    wide = jnp.concatenate([coarse] + beside, axis=1)
    beside = swaps(wide, ROWS)
    held = exchanged(stats, DEPTH)
    middle, stats = convolve(0, plane, block, whole, 1, at, held, gains, [wide] + beside, conv_one)
    held = exchanged(pooled(exchanged(stats, ROWS), own), DEPTH)
    last, stats = convolve(1, plane, block, whole, 0, at, held, gains, [middle], conv_two)
    held = exchanged(pooled(exchanged(stats, ROWS), own), DEPTH)
    mean, spread = pooled(held, plane)
    scale = gain / jnp.sqrt(spread / (plane * held.shape[0]) + 1e-05)
    features = leaky((last - mean) * scale + shift).astype(jnp.bfloat16)
    return jnp.transpose(features, (3, 0, 1, 2))


def solution(mesh):
    split = Mesh(mesh.devices.reshape(4, 4, 2, 16), ROWS + (DEPTH,))
    return jax.shard_map(
        on_device,
        mesh=split,
        in_specs=(P(None, ROWS, DEPTH, None), P(), P(), P(), P(), P()),
        out_specs=P(None, ROWS, DEPTH, None),
        check_vma=False,
    )
```

time: 130 us -> 123 us (0.946)
  blocking collectives: 40.8 us -> 90.7 us
  starting transfers between devices: 46.3 us -> 15.8 us
  waiting for transfers between devices: 26 us -> 3.57 us
  local copies, waits for them, and re-layouts: 5.95 us -> 3.29 us
    all_to_all x3 -> x6, blocking collectives: 40.8 us -> 90.7 us  [exchanged(): return lax.all_to_all(sent, axis, 0, 0)]
    all_to_all x3 -> x0, starting transfers between devices: 34.4 us -> none  [pooled(): held = lax.all_to_all(sent, axis, 0, 0)]
    all_to_all x3 -> x0, waiting for transfers between devices: 23.6 us -> none  [pooled(): held = lax.all_to_all(sent, axis, 0, 0)]
    ppermute x4, starting transfers between devices: 11.9 us -> 15.8 us  [swaps(): got.append(lax.ppermute(value, axis, pairs + [(j, i) for i, j in pairs]))]
    broadcast_in_dim x6, local copies, waits for them, and re-layouts: 1.88 us -> 0.06 us  [exchanged(): sent = jnp.broadcast_to(stats[None], (lax.axis_size(axis),) + stats.shape)]
  transfers between devices with their start and end apart: 7 -> 4, of which waited for: 5 -> 1; matrix products, arithmetic and copies ran while one was open for 2% -> 0% of each run, Pallas kernels for 0% -> 0%
where the time goes in v3:
time: 123 us
  blocking collectives  90.7 us (74%)
  starting transfers between devices  15.8 us (13%)
  Pallas kernels  8.08 us (7%)
  waiting for transfers between devices  3.57 us (3%)
  local copies, waits for them, and re-layouts  3.29 us (3%)
    all_to_all x6, blocking collectives, exchanged(): return lax.all_to_all(sent, axis, 0, 0)  90.7 us
    ppermute x4, starting transfers between devices, swaps(): got.append(lax.ppermute(value, axis, pairs + [(j, i) for i, j in pairs]))  15.8 us
    pallas_call x2, Pallas kernels, convolve(): pl.pallas_call(functools.partial(conv_kernel, norm, count, block, whole,...  8.08 us
    ppermute x4, waiting for transfers between devices, swaps(): got.append(lax.ppermute(value, axis, pairs + [(j, i) for i, j in pairs]))  3.57 us
  transfers between devices with their start and end apart: 4, of which 1 were waited for; matrix products, arithmetic and copies ran while one was open for 0% of the time, Pallas kernels for 0%

profile of v3, /device:TPU:1, one launch (start us, length us, event | category | flops | bytes accessed | tf_op | source)
XLA Modules:
  0.0 122.6 jit_solution(10504707146084352111)
XLA Ops:
  0.0 1.7 %copy.45 = bf16[64,4,4,256]{0,3,2,1:T(8,128)(2,1)S(1)} copy(bf16[64,4,4,256]{3,2,1,0:T(4,128)(2,1)} %param.6) | data formatting | bytes 1048576 | tf_op args[0]
  1.7 0.4 fusion.12
  2.0 0.7 collective-permute-start.1
  2.7 7.2 %collective-permute-start = (f32[2,2,128,128]{3,2,1,0:T(8,128)S(1)}, f32[2,2,128,128]{3,2,1,0:T(8,128)S(1)}, u32[]{:S(2)}, u32[]{:S(2)}) collective-permute-start(f32[2,2,128,128]{3,2,1,0:T(8,128)S(1)} %get-tuple-element.40), channel_id=1, source_target_pairs={{0,1},{2,3},{4,5},{6,7},{8,9},{10,11},{12,13},{14,15},{1,0},{3,2},... | collective-permute-start | bytes 786440 | tf_op jit(solution)/shard_map/ppermute | solution.py:22
  10.0 0.0 copy-start.2
  10.0 0.1 multiply_reduce_fusion
  10.1 0.6 copy-done.2
  10.7 0.1 copy-done.1
  10.8 0.0 collective-permute-done.1
  10.8 3.6 %collective-permute-done = f32[2,2,128,128]{3,2,1,0:T(8,128)S(1)} collective-permute-done((f32[2,2,128,128]{3,2,1,0:T(8,128)S(1)}, f32[2,2,128,128]{3,2,1,0:T(8,128)S(1)}, u32[]{:S(2)}, u32[]{:S(2)}) %collective-permute-start) | collective-permute-done | bytes 262176 | tf_op jit(solution)/shard_map/ppermute | solution.py:22
  14.4 0.1 pad_maximum_fusion.refs_0_
  14.4 5.9 %collective-permute-start.3 = (f32[2,6,128,128]{3,2,1,0:T(8,128)S(1)}, f32[2,6,128,128]{3,2,1,0:T(8,128)S(1)}, u32[]{:S(2)}, u32[]{:S(2)}) collective-permute-start(f32[2,6,128,128]{3,2,1,0:T(8,128)S(1)} %pad_maximum_fusion.refs_0_), channel_id=1, source_target_pairs={{16,32},{48,64},{80,96},{112,128},{144,160},{176,192},{208,224},{2... | collective-permute-start | bytes 2359304 | tf_op jit(solution)/shard_map/ppermute | solution.py:22
  20.4 1.9 %collective-permute-start.2 = (f32[2,6,128,128]{3,2,1,0:T(8,128)S(1)}, f32[2,6,128,128]{3,2,1,0:T(8,128)S(1)}, u32[]{:S(2)}, u32[]{:S(2)}) collective-permute-start(f32[2,6,128,128]{3,2,1,0:T(8,128)S(1)} %pad_maximum_fusion.refs_0_), channel_id=1, source_target_pairs={{0,16},{32,48},{64,80},{96,112},{128,144},{160,176},{192,208},{224... | collective-permute-start | bytes 2359304 | tf_op jit(solution)/shard_map/ppermute | solution.py:22
  22.3 0.1 pad_add_fusion.at
  22.4 14.4 %all_to_all.30 = f32[32,2,128]{2,1,0:T(2,128)S(1)} all-to-all(f32[32,2,128]{2,1,0:T(2,128)S(1)} %broadcast_in_dim.12), channel_id=1, replica_groups=mesh['x'=4,'y'=4,'core'=2,'z'=16] {'x','y','core'}, dimensions={0} | all-to-all | bytes 65536 | tf_op jit(solution)/shard_map/all_to_all | solution.py:28
  36.9 24.6 %all_to_all.31.held = f32[16,2,128]{2,1,0:T(2,128)S(1)} all-to-all(f32[16,2,128]{2,1,0:T(2,128)S(1)} %broadcast_in_dim.13), channel_id=1, replica_groups=mesh['x'=4,'y'=4,'core'=2,'z'=16] {'z'}, dimensions={0} | all-to-all | bytes 32768 | tf_op jit(solution)/shard_map/all_to_all | solution.py:28
  61.5 5.3 %shard_map.64 = (f32[4,4,128,128]{3,2,1,0:T(8,128)S(1)}, f32[2,128]{1,0:T(2,128)S(1)}) custom-call(s32[2]{0:T(128)S(1)} %pad_add_fusion.at, f32[16,2,128]{2,1,0:T(2,128)S(1)} %all_to_all.31.held, f32[2,3,128]{2,1,0:T(4,128)S(1)} %pad_maximum_fusion.1.gains, f32[2,6,128,128]{3,2,1,0:T(8,128)S(1)} %pad_maximum_fusion.refs_0_, ...), custom_call_target="tpu_custom_call" | custom-call | flops 1811939328 | bytes 2097152 | tf_op jit(solution)/shard_map/pallas_call | solution.py:145
  66.8 12.1 %all_to_all.32 = f32[32,2,128]{2,1,0:T(2,128)S(1)} all-to-all(f32[32,2,128]{2,1,0:T(2,128)S(1)} %broadcast_in_dim.14), channel_id=1, replica_groups=mesh['x'=4,'y'=4,'core'=2,'z'=16] {'x','y','core'}, dimensions={0} | all-to-all | bytes 65536 | tf_op jit(solution)/shard_map/all_to_all | solution.py:28
  79.1 13.9 %all_to_all.33.held = f32[16,2,128]{2,1,0:T(2,128)S(1)} all-to-all(f32[16,2,128]{2,1,0:T(2,128)S(1)} %broadcast_in_dim.15), channel_id=1, replica_groups=mesh['x'=4,'y'=4,'core'=2,'z'=16] {'z'}, dimensions={0} | all-to-all | bytes 32768 | tf_op jit(solution)/shard_map/all_to_all | solution.py:28
  92.9 2.8 %shard_map.65 = (f32[2,2,128,128]{3,2,1,0:T(8,128)S(1)}, f32[2,128]{1,0:T(2,128)S(1)}) custom-call(s32[2]{0:T(128)S(1)} %pad_add_fusion.at, f32[16,2,128]{2,1,0:T(2,128)S(1)} %all_to_all.33.held, f32[2,3,128]{2,1,0:T(4,128)S(1)} %pad_maximum_fusion.1.gains, f32[4,4,128,128]{3,2,1,0:T(8,128)S(1)} %get-tuple-element.18.refs_0_, bf16[3,3,128,384]{3,2,1,0:T(8,128)(2,1)} %refs_1_.1), custom_call_target="tpu_custom_call" | custom-call | flops 452984832 | bytes 2097152 | tf_op jit(solution)/shard_map/pallas_call | solution.py:145
  95.7 11.9 %all_to_all.34 = f32[32,2,128]{2,1,0:T(2,128)S(1)} all-to-all(f32[32,2,128]{2,1,0:T(2,128)S(1)} %broadcast_in_dim.16), channel_id=1, replica_groups=mesh['x'=4,'y'=4,'core'=2,'z'=16] {'x','y','core'}, dimensions={0} | all-to-all | bytes 65536 | tf_op jit(solution)/shard_map/all_to_all | solution.py:28
  107.7 13.9 %all_to_all.35 = f32[16,2,128]{2,1,0:T(2,128)S(1)} all-to-all(f32[16,2,128]{2,1,0:T(2,128)S(1)} %broadcast_in_dim.17), channel_id=1, replica_groups=mesh['x'=4,'y'=4,'core'=2,'z'=16] {'z'}, dimensions={0} | all-to-all | bytes 32768 | tf_op jit(solution)/shard_map/all_to_all | solution.py:28
  121.7 0.1 fusion.2
  121.8 0.8 copy.54
  (35 shorter events, 0.4 us)
Async XLA Ops:
  0.0 1.7 %copy-start = (bf16[128,64,2,2,2]{0,4,3,2,1:T(2,128)(2,1)S(1)}, bf16[128,64,2,2,2]{0,4,3,2,1:T(2,128)(2,1)}, u32[]{:S(2)}) copy-start(bf16[128,64,2,2,2]{0,4,3,2,1:T(2,128)(2,1)} %param.7) | copy-start | bytes 393220
  2.0 8.8 %collective-permute-start.1 = (f32[2,2,128,128]{3,2,1,0:T(8,128)S(1)}, f32[2,2,128,128]{3,2,1,0:T(8,128)S(1)}, u32[]{:S(2)}, u32[]{:S(2)}) collective-permute-start(f32[2,2,128,128]{3,2,1,0:T(8,128)S(1)} %get-tuple-element.40), channel_id=1, source_target_pairs={{1,2},{3,4},{5,6},{7,8},{9,10},{11,12},{13,14},{2,1},{4,3},{6,5},{... | collective-permute-start | bytes 786440 | tf_op jit(solution)/shard_map/ppermute | solution.py:22
  2.7 11.6 %collective-permute-start = (f32[2,2,128,128]{3,2,1,0:T(8,128)S(1)}, f32[2,2,128,128]{3,2,1,0:T(8,128)S(1)}, u32[]{:S(2)}, u32[]{:S(2)}) collective-permute-start(f32[2,2,128,128]{3,2,1,0:T(8,128)S(1)} %get-tuple-element.40), channel_id=1, source_target_pairs={{0,1},{2,3},{4,5},{6,7},{8,9},{10,11},{12,13},{14,15},{1,0},{3,2},... | collective-permute-start | bytes 786440 | tf_op jit(solution)/shard_map/ppermute | solution.py:22
  10.0 0.7 copy-start.2
  10.1 0.7 copy-start.1
  14.4 47.0 %collective-permute-start.3 = (f32[2,6,128,128]{3,2,1,0:T(8,128)S(1)}, f32[2,6,128,128]{3,2,1,0:T(8,128)S(1)}, u32[]{:S(2)}, u32[]{:S(2)}) collective-permute-start(f32[2,6,128,128]{3,2,1,0:T(8,128)S(1)} %pad_maximum_fusion.refs_0_), channel_id=1, source_target_pairs={{16,32},{48,64},{80,96},{112,128},{144,160},{176,192},{208,224},{2... | collective-permute-start | bytes 2359304 | tf_op jit(solution)/shard_map/ppermute | solution.py:22
  20.4 41.1 %collective-permute-start.2 = (f32[2,6,128,128]{3,2,1,0:T(8,128)S(1)}, f32[2,6,128,128]{3,2,1,0:T(8,128)S(1)}, u32[]{:S(2)}, u32[]{:S(2)}) collective-permute-start(f32[2,6,128,128]{3,2,1,0:T(8,128)S(1)} %pad_maximum_fusion.refs_0_), channel_id=1, source_target_pairs={{0,16},{32,48},{64,80},{96,112},{128,144},{160,176},{192,208},{224... | collective-permute-start | bytes 2359304 | tf_op jit(solution)/shard_map/ppermute | solution.py:22

commit v4 on v3

--- a/solution.py
+++ b/solution.py
@@ -187,9 +187,11 @@
     at = jnp.stack([lax.axis_index(ROWS), lax.axis_index(DEPTH)])
     gains = jnp.stack([norm_gain, norm_shift])
 
-    stats, at, gains, gain, shift = lax.optimization_barrier(
-        (local_moments(coarse), at, gains, norm_gain[2], norm_shift[2])
-    )
+    coarse, at, gains, gain, shift = lax.optimization_barrier(
+        (coarse, at, gains, norm_gain[2], norm_shift[2])
+    )
+
+    stats = local_moments(coarse)
     beside = swaps(coarse, DEPTH)
     stats = pooled(exchanged(stats, ROWS), own)
     wide = jnp.concatenate([coarse] + beside, axis=1)

time: 123 us -> 124 us (level)
  no operation moved by 1% of the time
where the time goes in v4:
time: 124 us; the launch traced here: 123 us
  blocking collectives  90.7 us (73%)
  starting transfers between devices  15.8 us (13%)
  Pallas kernels  8.08 us (7%)
  waiting for transfers between devices  4.23 us (3%)
  local copies, waits for them, and re-layouts  3.25 us (3%)
    all_to_all x6, blocking collectives, exchanged(): return lax.all_to_all(sent, axis, 0, 0)  90.7 us
    ppermute x4, starting transfers between devices, swaps(): got.append(lax.ppermute(value, axis, pairs + [(j, i) for i, j in pairs]))  15.8 us
    pallas_call x2, Pallas kernels, convolve(): pl.pallas_call(functools.partial(conv_kernel, norm, count, block, whole,...  8.08 us
    ppermute x4, waiting for transfers between devices, swaps(): got.append(lax.ppermute(value, axis, pairs + [(j, i) for i, j in pairs]))  4.23 us
  transfers between devices with their start and end apart: 4, of which 1 were waited for; matrix products, arithmetic and copies ran while one was open for 0% of the time, Pallas kernels for 0%

profile of v4, /device:TPU:1, one launch (start us, length us, event | category | flops | bytes accessed | tf_op | source)
XLA Modules:
  0.0 123.2 jit_solution(1640864681224020064)
XLA Ops:
  0.0 1.7 %copy.45 = bf16[64,4,4,256]{0,3,2,1:T(8,128)(2,1)S(1)} copy(bf16[64,4,4,256]{3,2,1,0:T(4,128)(2,1)} %param.6) | data formatting | bytes 1048576 | tf_op args[0]
  1.7 0.0 copy-start.1
  1.7 0.1 pad_add_fusion.at
  1.8 0.6 copy-done.1
  2.4 0.4 convolution_bitcast_fusion
  2.8 0.7 collective-permute-start.1
  3.4 7.2 %collective-permute-start = (f32[2,2,128,128]{3,2,1,0:T(8,128)S(1)}, f32[2,2,128,128]{3,2,1,0:T(8,128)S(1)}, u32[]{:S(2)}, u32[]{:S(2)}) collective-permute-start(f32[2,2,128,128]{3,2,1,0:T(8,128)S(1)} %convolution_bitcast_fusion), channel_id=1, source_target_pairs={{0,1},{2,3},{4,5},{6,7},{8,9},{10,11},{12,13},{14,15},{1,0},{3,2},... | collective-permute-start | bytes 786440 | tf_op jit(solution)/shard_map/ppermute | solution.py:22
  10.7 0.1 reduce_sum.90
  10.8 0.1 constant_dynamic-update-slice_fusion.2
  10.9 4.2 %collective-permute-done = f32[2,2,128,128]{3,2,1,0:T(8,128)S(1)} collective-permute-done((f32[2,2,128,128]{3,2,1,0:T(8,128)S(1)}, f32[2,2,128,128]{3,2,1,0:T(8,128)S(1)}, u32[]{:S(2)}, u32[]{:S(2)}) %collective-permute-start) | collective-permute-done | bytes 262176 | tf_op jit(solution)/shard_map/ppermute | solution.py:22
  15.1 5.9 %collective-permute-start.3 = (f32[2,6,128,128]{3,2,1,0:T(8,128)S(1)}, f32[2,6,128,128]{3,2,1,0:T(8,128)S(1)}, u32[]{:S(2)}, u32[]{:S(2)}) collective-permute-start(f32[2,6,128,128]{3,2,1,0:T(8,128)S(1)} %constant_dynamic-update-slice_fusion.refs_0_), channel_id=1, source_target_pairs={{16,32},{48,64},{80,96},{112,128},{144,160},{176,192},{208,224},{2... | collective-permute-start | bytes 2359304 | tf_op jit(solution)/shard_map/ppermute | solution.py:22
  21.1 1.9 %collective-permute-start.2 = (f32[2,6,128,128]{3,2,1,0:T(8,128)S(1)}, f32[2,6,128,128]{3,2,1,0:T(8,128)S(1)}, u32[]{:S(2)}, u32[]{:S(2)}) collective-permute-start(f32[2,6,128,128]{3,2,1,0:T(8,128)S(1)} %constant_dynamic-update-slice_fusion.refs_0_), channel_id=1, source_target_pairs={{0,16},{32,48},{64,80},{96,112},{128,144},{160,176},{192,208},{224... | collective-permute-start | bytes 2359304 | tf_op jit(solution)/shard_map/ppermute | solution.py:22
  23.1 14.4 %all_to_all.30 = f32[32,2,128]{2,1,0:T(2,128)S(1)} all-to-all(f32[32,2,128]{2,1,0:T(2,128)S(1)} %broadcast_in_dim.12), channel_id=1, replica_groups=mesh['x'=4,'y'=4,'core'=2,'z'=16] {'x','y','core'}, dimensions={0} | all-to-all | bytes 65536 | tf_op jit(solution)/shard_map/all_to_all | solution.py:28
  37.5 24.6 %all_to_all.31.held = f32[16,2,128]{2,1,0:T(2,128)S(1)} all-to-all(f32[16,2,128]{2,1,0:T(2,128)S(1)} %broadcast_in_dim.13), channel_id=1, replica_groups=mesh['x'=4,'y'=4,'core'=2,'z'=16] {'z'}, dimensions={0} | all-to-all | bytes 32768 | tf_op jit(solution)/shard_map/all_to_all | solution.py:28
  62.1 0.0 collective-permute-done.3.refs_2_
  62.1 0.0 collective-permute-done.2.refs_1_
  62.1 5.3 %shard_map.64 = (f32[4,4,128,128]{3,2,1,0:T(8,128)S(1)}, f32[2,128]{1,0:T(2,128)S(1)}) custom-call(s32[2]{0:T(128)S(1)} %pad_add_fusion.at, f32[16,2,128]{2,1,0:T(2,128)S(1)} %all_to_all.31.held, f32[2,3,128]{2,1,0:T(4,128)S(1)} %pad_maximum_fusion.gains, f32[2,6,128,128]{3,2,1,0:T(8,128)S(1)} %constant_dynamic-update-slice_fusion.refs_0_, ...), custom_call_target="tpu_custom_call" | custom-call | flops 1811939328 | bytes 2097152 | tf_op jit(solution)/shard_map/pallas_call | solution.py:145
  67.5 12.1 %all_to_all.32 = f32[32,2,128]{2,1,0:T(2,128)S(1)} all-to-all(f32[32,2,128]{2,1,0:T(2,128)S(1)} %broadcast_in_dim.14), channel_id=1, replica_groups=mesh['x'=4,'y'=4,'core'=2,'z'=16] {'x','y','core'}, dimensions={0} | all-to-all | bytes 65536 | tf_op jit(solution)/shard_map/all_to_all | solution.py:28
  79.7 13.9 %all_to_all.33.held = f32[16,2,128]{2,1,0:T(2,128)S(1)} all-to-all(f32[16,2,128]{2,1,0:T(2,128)S(1)} %broadcast_in_dim.15), channel_id=1, replica_groups=mesh['x'=4,'y'=4,'core'=2,'z'=16] {'z'}, dimensions={0} | all-to-all | bytes 32768 | tf_op jit(solution)/shard_map/all_to_all | solution.py:28
  93.6 2.8 %shard_map.65 = (f32[2,2,128,128]{3,2,1,0:T(8,128)S(1)}, f32[2,128]{1,0:T(2,128)S(1)}) custom-call(s32[2]{0:T(128)S(1)} %pad_add_fusion.at, f32[16,2,128]{2,1,0:T(2,128)S(1)} %all_to_all.33.held, f32[2,3,128]{2,1,0:T(4,128)S(1)} %pad_maximum_fusion.gains, f32[4,4,128,128]{3,2,1,0:T(8,128)S(1)} %get-tuple-element.18.refs_0_, bf16[3,3,128,384]{3,2,1,0:T(8,128)(2,1)} %refs_1_.1), custom_call_target="tpu_custom_call" | custom-call | flops 452984832 | bytes 2097152 | tf_op jit(solution)/shard_map/pallas_call | solution.py:145
  96.4 11.9 %all_to_all.34 = f32[32,2,128]{2,1,0:T(2,128)S(1)} all-to-all(f32[32,2,128]{2,1,0:T(2,128)S(1)} %broadcast_in_dim.16), channel_id=1, replica_groups=mesh['x'=4,'y'=4,'core'=2,'z'=16] {'x','y','core'}, dimensions={0} | all-to-all | bytes 65536 | tf_op jit(solution)/shard_map/all_to_all | solution.py:28
  108.4 13.9 %all_to_all.35 = f32[16,2,128]{2,1,0:T(2,128)S(1)} all-to-all(f32[16,2,128]{2,1,0:T(2,128)S(1)} %broadcast_in_dim.17), channel_id=1, replica_groups=mesh['x'=4,'y'=4,'core'=2,'z'=16] {'z'}, dimensions={0} | all-to-all | bytes 32768 | tf_op jit(solution)/shard_map/all_to_all | solution.py:28
  122.3 0.1 fusion.2
  122.4 0.8 copy.54
  (37 shorter events, 0.5 us)
Async XLA Ops:
  0.0 2.4 %copy-start = (bf16[128,64,2,2,2]{0,4,3,2,1:T(2,128)(2,1)S(1)}, bf16[128,64,2,2,2]{0,4,3,2,1:T(2,128)(2,1)}, u32[]{:S(2)}) copy-start(bf16[128,64,2,2,2]{0,4,3,2,1:T(2,128)(2,1)} %param.7) | copy-start | bytes 393220
  0.0 1.8 %copy-start.2 = (f32[3,128]{1,0:T(4,128)S(1)}, f32[3,128]{1,0:T(4,128)}, u32[]{:S(2)}) copy-start(f32[3,128]{1,0:T(4,128)} %param.10) | copy-start | bytes 4612
  1.7 0.7 copy-start.1
  2.8 12.3 %collective-permute-start.1 = (f32[2,2,128,128]{3,2,1,0:T(8,128)S(1)}, f32[2,2,128,128]{3,2,1,0:T(8,128)S(1)}, u32[]{:S(2)}, u32[]{:S(2)}) collective-permute-start(f32[2,2,128,128]{3,2,1,0:T(8,128)S(1)} %convolution_bitcast_fusion), channel_id=1, source_target_pairs={{1,2},{3,4},{5,6},{7,8},{9,10},{11,12},{13,14},{2,1},{4,3},{6,5},{... | collective-permute-start | bytes 786440 | tf_op jit(solution)/shard_map/ppermute | solution.py:22
  3.4 11.6 %collective-permute-start = (f32[2,2,128,128]{3,2,1,0:T(8,128)S(1)}, f32[2,2,128,128]{3,2,1,0:T(8,128)S(1)}, u32[]{:S(2)}, u32[]{:S(2)}) collective-permute-start(f32[2,2,128,128]{3,2,1,0:T(8,128)S(1)} %convolution_bitcast_fusion), channel_id=1, source_target_pairs={{0,1},{2,3},{4,5},{6,7},{8,9},{10,11},{12,13},{14,15},{1,0},{3,2},... | collective-permute-start | bytes 786440 | tf_op jit(solution)/shard_map/ppermute | solution.py:22
  15.1 47.0 %collective-permute-start.3 = (f32[2,6,128,128]{3,2,1,0:T(8,128)S(1)}, f32[2,6,128,128]{3,2,1,0:T(8,128)S(1)}, u32[]{:S(2)}, u32[]{:S(2)}) collective-permute-start(f32[2,6,128,128]{3,2,1,0:T(8,128)S(1)} %constant_dynamic-update-slice_fusion.refs_0_), channel_id=1, source_target_pairs={{16,32},{48,64},{80,96},{112,128},{144,160},{176,192},{208,224},{2... | collective-permute-start | bytes 2359304 | tf_op jit(solution)/shard_map/ppermute | solution.py:22
  21.1 41.0 %collective-permute-start.2 = (f32[2,6,128,128]{3,2,1,0:T(8,128)S(1)}, f32[2,6,128,128]{3,2,1,0:T(8,128)S(1)}, u32[]{:S(2)}, u32[]{:S(2)}) collective-permute-start(f32[2,6,128,128]{3,2,1,0:T(8,128)S(1)} %constant_dynamic-update-slice_fusion.refs_0_), channel_id=1, source_target_pairs={{0,16},{32,48},{64,80},{96,112},{128,144},{160,176},{192,208},{224... | collective-permute-start | bytes 2359304 | tf_op jit(solution)/shard_map/ppermute | solution.py:22

commit v5 on v4

v5 whole, which is shorter than its diff:
```python
import functools

import jax
import jax.numpy as jnp
from jax import lax
from jax.experimental import pallas as pl
from jax.experimental.pallas import tpu as pltpu
from jax.sharding import Mesh
from jax.sharding import PartitionSpec as P


ROWS = ("x", "y", "core")
DEPTH = "z"


def swaps(value, axis):
    count = lax.axis_size(axis)
    even = [(i, i + 1) for i in range(0, count - 1, 2)]
    odd = [(i, i + 1) for i in range(1, count - 1, 2)]
    got = []
    for pairs in (even, odd):
        got.append(lax.ppermute(value, axis, pairs + [(j, i) for i, j in pairs]))
    return got


def exchanged(stats, axis):
    sent = jnp.broadcast_to(stats[None], (lax.axis_size(axis),) + stats.shape)
    return lax.all_to_all(sent, axis, 0, 0)


def pooled(held, count):
    mean = jnp.mean(held[:, 0], axis=0)
    apart = held[:, 0] - mean
    spread = jnp.sum(held[:, 1] + count * (apart * apart), axis=0)
    return jnp.stack([mean, spread])


def affine(held, count, gain, shift):
    parts = held.shape[0]
    means = [held[part, 0:1, :] for part in range(parts)]
    mean = sum(means) / parts
    spread = sum(
        held[part, 1:2, :] + count * ((means[part] - mean) * (means[part] - mean))
        for part in range(parts)
    )
    return mean, gain / jnp.sqrt(spread / (count * parts) + 1e-05), shift


def leaky(value):
    return jnp.where(value >= 0.0, value, 0.01 * value)


def orders(at, own, swapped):
    if not swapped:
        return [(0, 0, own)]
    odd = lax.rem(at, 2)
    return [(0, own, own), (own, (1 - odd) * 2 * own, own), (2 * own, odd * 2 * own, own)]


def conv_kernel(norm, count, block, whole, rim, swapped, at, held, gains, shifts, *refs):
    pieces = 3 if swapped else 1
    fields, (source, out, stats, gain, moved, stacked, weight, arrived) = refs[:pieces], refs[pieces:]
    fetch = pltpu.make_async_copy(source, weight, arrived)
    fetch.start()
    length, channels = fields[0].shape[2:]
    rows, depth = len(fields) * fields[0].shape[0], fields[0].shape[1]

    mean, scale, shift = affine(held, count, gains[norm : norm + 1, :], shifts[norm : norm + 1, :])
    row_at = at[0] * block[0] - (rows - block[0]) // 2
    depth_at = at[1] * block[1] - (depth - block[1]) // 2
    row_groups = orders(at[0], block[0] if swapped else rows, swapped)
    depth_groups = orders(at[1], block[1] if swapped else depth, swapped)
    for piece, (_, to_row, row_count) in enumerate(row_groups):
        for from_cell, to_cell, cell_count in depth_groups:
            for i in range(row_count):
                for j in range(cell_count):
                    row, cell = to_row + i, to_cell + j
                    y, z = row_at + row, depth_at + cell
                    here = (y >= 0) & (y < whole[0]) & (z >= 0) & (z < whole[1])
                    keep = jnp.where(here, 1.0, 0.0)
                    value = (fields[piece][i, from_cell + j] - mean) * (scale * keep) + shift * keep
                    value = jnp.maximum(value, 0.01 * value)
                    stacked[row * depth + cell] = value.astype(jnp.bfloat16)

    fetch.wait()
    cells = depth - 2
    taps = jnp.concatenate(
        [
            jnp.concatenate(
                [weight[tap // 3, tap % 3, :, part * channels : (part + 1) * channels] for tap in range(9)],
                axis=1,
            )
            for part in range(3)
        ],
        axis=0,
    )
    place = lax.broadcasted_iota(jnp.int32, (length, channels), 0)
    for row in range(rows - 2):
        taken = jnp.concatenate(
            [
                stacked[pl.ds((row + tap // 3) * depth + tap % 3, cells)].reshape(cells * length, channels)
                for tap in range(9)
            ],
            axis=1,
        )
        product = lax.dot_general(
            taken, taps, (((1,), (1,)), ((), ())), preferred_element_type=jnp.float32
        )
        for cell in range(cells):
            before, here, after = (
                product[cell * length : (cell + 1) * length, part * channels : (part + 1) * channels]
                for part in range(3)
            )
            before = jnp.where(place > 0, pltpu.roll(before, 1, 0), 0.0)
            after = jnp.where(place < length - 1, pltpu.roll(after, length - 1, 0), 0.0)
            out[row, cell] = before + here + after

    inner = [
        out[row, cell]
        for row in range(rim, rows - 2 - rim)
        for cell in range(rim, cells - rim)
    ]
    middle = sum(jnp.sum(plane, axis=0, keepdims=True) for plane in inner) / (len(inner) * length)
    apart = [plane - middle for plane in inner]
    spread = sum(jnp.sum(plane * plane, axis=0, keepdims=True) for plane in apart)
    stats[0:1, :] = middle
    stats[1:2, :] = spread
    gain[...] = gains[norm + 1 : norm + 2, :]
    moved[...] = shifts[norm + 1 : norm + 2, :]


def convolve(norm, count, block, whole, rim, at, held, gains, shifts, fields, weight):
    pieces = len(fields)
    rows = pieces * fields[0].shape[0]
    depth, length, channels = fields[0].shape[1:]
    in_vmem = pl.BlockSpec(memory_space=pltpu.VMEM)
    flops = 2 * (rows - 2) * (depth - 2) * length * channels * channels * 27
    return pl.pallas_call(
        functools.partial(conv_kernel, norm, count, block, whole, rim, pieces == 3),
        out_shape=(
            jax.ShapeDtypeStruct((rows - 2, depth - 2, length, channels), jnp.float32),
            jax.ShapeDtypeStruct((2, channels), jnp.float32),
            jax.ShapeDtypeStruct((1, channels), jnp.float32),
            jax.ShapeDtypeStruct((1, channels), jnp.float32),
        ),
        in_specs=[pl.BlockSpec(memory_space=pltpu.SMEM)]
        + [in_vmem] * (3 + pieces)
        + [pl.BlockSpec(memory_space=pltpu.HBM)],
        out_specs=(in_vmem,) * 4,
        scratch_shapes=[
            pltpu.VMEM((rows * depth, length, channels), jnp.bfloat16),
            pltpu.VMEM(weight.shape, weight.dtype),
            pltpu.SemaphoreType.DMA(()),
        ],
        compiler_params=pltpu.CompilerParams(vmem_limit_bytes=16 << 20),
        cost_estimate=pl.CostEstimate(flops=flops, bytes_accessed=2 << 20, transcendentals=0),
    )(at, held, gains, shifts, *fields, pltpu.with_memory_space_constraint(weight, pltpu.HBM))


def strided(volume, down_weight):
    blocks = volume.reshape(
        volume.shape[0], volume.shape[1] // 2, 2, volume.shape[2] // 2, 2, volume.shape[3] // 2, 2
    )
    return jnp.einsum(
        "oiabc,iyazbxc->yzxo", down_weight, blocks, preferred_element_type=jnp.float32
    )


def local_moments(inner):
    mean = jnp.mean(inner, axis=(0, 1, 2))
    centered = inner - mean
    return jnp.stack([mean, jnp.sum(centered * centered, axis=(0, 1, 2))])


def on_device(volume, down_weight, conv_one, conv_two, norm_gain, norm_shift):
    coarse = strided(volume, down_weight)
    rows, depth, length = coarse.shape[:3]
    block = (rows, depth)
    whole = (rows * lax.axis_size(ROWS), depth * lax.axis_size(DEPTH))
    own = float(rows * depth * length)
    plane = own * lax.axis_size(ROWS)
    at = jnp.stack([lax.axis_index(ROWS), lax.axis_index(DEPTH)])
    coarse, at = lax.optimization_barrier((coarse, at))

    stats = local_moments(coarse)
    beside = swaps(coarse, DEPTH)
    stats = pooled(exchanged(stats, ROWS), own)
    wide = jnp.concatenate([coarse] + beside, axis=1)
    beside = swaps(wide, ROWS)
    held = exchanged(stats, DEPTH)
    middle, stats, _, _ = convolve(0, plane, block, whole, 1, at, held, norm_gain, norm_shift, [wide] + beside, conv_one)
    held = exchanged(pooled(exchanged(stats, ROWS), own), DEPTH)
    last, stats, gain, shift = convolve(1, plane, block, whole, 0, at, held, norm_gain, norm_shift, [middle], conv_two)
    held = exchanged(pooled(exchanged(stats, ROWS), own), DEPTH)
    mean, spread = pooled(held, plane)
    scale = gain[0] / jnp.sqrt(spread / (plane * held.shape[0]) + 1e-05)
    features = leaky((last - mean) * scale + shift[0]).astype(jnp.bfloat16)
    return jnp.transpose(features, (3, 0, 1, 2))


def solution(mesh):
    split = Mesh(mesh.devices.reshape(4, 4, 2, 16), ROWS + (DEPTH,))
    return jax.shard_map(
        on_device,
        mesh=split,
        in_specs=(P(None, ROWS, DEPTH, None), P(), P(), P(), P(), P()),
        out_specs=P(None, ROWS, DEPTH, None),
        check_vma=False,
    )
```

time: 124 us -> 123 us (level)
  no operation moved by 1% of the time
where the time goes in v5:
time: 123 us
  blocking collectives  90.7 us (74%)
  starting transfers between devices  15.8 us (13%)
  Pallas kernels  8.04 us (7%)
  waiting for transfers between devices  4.22 us (3%)
  local copies, waits for them, and re-layouts  2.65 us (2%)
    all_to_all x6, blocking collectives, exchanged(): return lax.all_to_all(sent, axis, 0, 0)  90.7 us
    ppermute x4, starting transfers between devices, swaps(): got.append(lax.ppermute(value, axis, pairs + [(j, i) for i, j in pairs]))  15.8 us
    pallas_call x2, Pallas kernels, convolve(): pl.pallas_call(functools.partial(conv_kernel, norm, count, block, whole,...  8.04 us
    ppermute x4, waiting for transfers between devices, swaps(): got.append(lax.ppermute(value, axis, pairs + [(j, i) for i, j in pairs]))  4.22 us
  transfers between devices with their start and end apart: 4, of which 1 were waited for; matrix products, arithmetic and copies ran while one was open for 0% of the time, Pallas kernels for 0%

profile of v5, /device:TPU:1, one launch (start us, length us, event | category | flops | bytes accessed | tf_op | source)
XLA Modules:
  0.0 122.6 jit_solution(7466742907167215500)
XLA Ops:
  0.0 1.7 %copy.45 = bf16[64,4,4,256]{0,3,2,1:T(8,128)(2,1)S(1)} copy(bf16[64,4,4,256]{3,2,1,0:T(4,128)(2,1)} %param.6) | data formatting | bytes 1048576 | tf_op args[0]
  1.7 0.1 pad_add_fusion.at
  1.8 0.4 convolution_bitcast_fusion
  2.1 0.7 collective-permute-start.1
  2.8 7.2 %collective-permute-start = (f32[2,2,128,128]{3,2,1,0:T(8,128)S(1)}, f32[2,2,128,128]{3,2,1,0:T(8,128)S(1)}, u32[]{:S(2)}, u32[]{:S(2)}) collective-permute-start(f32[2,2,128,128]{3,2,1,0:T(8,128)S(1)} %convolution_bitcast_fusion), channel_id=1, source_target_pairs={{0,1},{2,3},{4,5},{6,7},{8,9},{10,11},{12,13},{14,15},{1,0},{3,2},... | collective-permute-start | bytes 786440 | tf_op jit(solution)/shard_map/ppermute | solution.py:22
  10.0 0.1 reduce_sum.90
  10.1 0.1 constant_dynamic-update-slice_fusion.2
  10.2 4.2 %collective-permute-done = f32[2,2,128,128]{3,2,1,0:T(8,128)S(1)} collective-permute-done((f32[2,2,128,128]{3,2,1,0:T(8,128)S(1)}, f32[2,2,128,128]{3,2,1,0:T(8,128)S(1)}, u32[]{:S(2)}, u32[]{:S(2)}) %collective-permute-start) | collective-permute-done | bytes 262176 | tf_op jit(solution)/shard_map/ppermute | solution.py:22
  14.5 5.9 %collective-permute-start.3 = (f32[2,6,128,128]{3,2,1,0:T(8,128)S(1)}, f32[2,6,128,128]{3,2,1,0:T(8,128)S(1)}, u32[]{:S(2)}, u32[]{:S(2)}) collective-permute-start(f32[2,6,128,128]{3,2,1,0:T(8,128)S(1)} %constant_dynamic-update-slice_fusion.refs_0_), channel_id=1, source_target_pairs={{16,32},{48,64},{80,96},{112,128},{144,160},{176,192},{208,224},{2... | collective-permute-start | bytes 2359304 | tf_op jit(solution)/shard_map/ppermute | solution.py:22
  20.4 1.9 %collective-permute-start.2 = (f32[2,6,128,128]{3,2,1,0:T(8,128)S(1)}, f32[2,6,128,128]{3,2,1,0:T(8,128)S(1)}, u32[]{:S(2)}, u32[]{:S(2)}) collective-permute-start(f32[2,6,128,128]{3,2,1,0:T(8,128)S(1)} %constant_dynamic-update-slice_fusion.refs_0_), channel_id=1, source_target_pairs={{0,16},{32,48},{64,80},{96,112},{128,144},{160,176},{192,208},{224... | collective-permute-start | bytes 2359304 | tf_op jit(solution)/shard_map/ppermute | solution.py:22
  22.4 14.4 %all_to_all.30 = f32[32,2,128]{2,1,0:T(2,128)S(1)} all-to-all(f32[32,2,128]{2,1,0:T(2,128)S(1)} %broadcast_in_dim.12), channel_id=1, replica_groups=mesh['x'=4,'y'=4,'core'=2,'z'=16] {'x','y','core'}, dimensions={0} | all-to-all | bytes 65536 | tf_op jit(solution)/shard_map/all_to_all | solution.py:28
  36.9 0.0 copy-start.1
  36.9 0.0 copy-start.2
  36.9 24.6 %all_to_all.31.held = f32[16,2,128]{2,1,0:T(2,128)S(1)} all-to-all(f32[16,2,128]{2,1,0:T(2,128)S(1)} %broadcast_in_dim.13), channel_id=1, replica_groups=mesh['x'=4,'y'=4,'core'=2,'z'=16] {'z'}, dimensions={0} | all-to-all | bytes 32768 | tf_op jit(solution)/shard_map/all_to_all | solution.py:28
  61.5 0.0 collective-permute-done.3.refs_2_
  61.5 0.0 collective-permute-done.2.refs_1_
  61.5 5.4 %shard_map.64 = (f32[4,4,128,128]{3,2,1,0:T(8,128)S(1)}, f32[2,128]{1,0:T(2,128)S(1)}, f32[1,128]{1,0:T(1,128)}, f32[1,128]{1,0:T(1,128)}) custom-call(s32[2]{0:T(128)S(1)} %pad_add_fusion.at, f32[16,2,128]{2,1,0:T(2,128)S(1)} %all_to_all.31.held, f32[3,128]{1,0:T(4,128)S(1)} %copy-done.1, f32[3,128]{1,0:T(4,128)S(1)} %copy-done.2, ...), custom_call_target="tpu_custom_call" | custom-call | flops 1811939328 | bytes 2097152 | tf_op jit(solution)/shard_map/pallas_call | solution.py:138
  67.0 12.1 %all_to_all.32 = f32[32,2,128]{2,1,0:T(2,128)S(1)} all-to-all(f32[32,2,128]{2,1,0:T(2,128)S(1)} %broadcast_in_dim.14), channel_id=1, replica_groups=mesh['x'=4,'y'=4,'core'=2,'z'=16] {'x','y','core'}, dimensions={0} | all-to-all | bytes 65536 | tf_op jit(solution)/shard_map/all_to_all | solution.py:28
  79.2 13.9 %all_to_all.33.held = f32[16,2,128]{2,1,0:T(2,128)S(1)} all-to-all(f32[16,2,128]{2,1,0:T(2,128)S(1)} %broadcast_in_dim.15), channel_id=1, replica_groups=mesh['x'=4,'y'=4,'core'=2,'z'=16] {'z'}, dimensions={0} | all-to-all | bytes 32768 | tf_op jit(solution)/shard_map/all_to_all | solution.py:28
  93.1 2.6 %shard_map.65 = (f32[2,2,128,128]{3,2,1,0:T(8,128)S(1)}, f32[2,128]{1,0:T(2,128)S(1)}, f32[1,128]{1,0:T(1,128)S(1)}, f32[1,128]{1,0:T(1,128)S(1)}) custom-call(s32[2]{0:T(128)S(1)} %pad_add_fusion.at, f32[16,2,128]{2,1,0:T(2,128)S(1)} %all_to_all.33.held, f32[3,128]{1,0:T(4,128)S(1)} %copy-done.1, f32[3,128]{1,0:T(4,128)S(1)} %copy-done.2, ...), custom_call_target="tpu_custom_call" | custom-call | flops 452984832 | bytes 2097152 | tf_op jit(solution)/shard_map/pallas_call | solution.py:138
  95.7 11.9 %all_to_all.34 = f32[32,2,128]{2,1,0:T(2,128)S(1)} all-to-all(f32[32,2,128]{2,1,0:T(2,128)S(1)} %broadcast_in_dim.16), channel_id=1, replica_groups=mesh['x'=4,'y'=4,'core'=2,'z'=16] {'x','y','core'}, dimensions={0} | all-to-all | bytes 65536 | tf_op jit(solution)/shard_map/all_to_all | solution.py:28
  107.8 13.9 %all_to_all.35 = f32[16,2,128]{2,1,0:T(2,128)S(1)} all-to-all(f32[16,2,128]{2,1,0:T(2,128)S(1)} %broadcast_in_dim.17), channel_id=1, replica_groups=mesh['x'=4,'y'=4,'core'=2,'z'=16] {'z'}, dimensions={0} | all-to-all | bytes 32768 | tf_op jit(solution)/shard_map/all_to_all | solution.py:28
  121.7 0.1 fusion.2
  121.8 0.8 copy.54
  (35 shorter events, 0.5 us)
Async XLA Ops:
  0.0 1.8 %copy-start = (bf16[128,64,2,2,2]{0,4,3,2,1:T(2,128)(2,1)S(1)}, bf16[128,64,2,2,2]{0,4,3,2,1:T(2,128)(2,1)}, u32[]{:S(2)}) copy-start(bf16[128,64,2,2,2]{0,4,3,2,1:T(2,128)(2,1)} %param.7) | copy-start | bytes 393220
  2.1 12.3 %collective-permute-start.1 = (f32[2,2,128,128]{3,2,1,0:T(8,128)S(1)}, f32[2,2,128,128]{3,2,1,0:T(8,128)S(1)}, u32[]{:S(2)}, u32[]{:S(2)}) collective-permute-start(f32[2,2,128,128]{3,2,1,0:T(8,128)S(1)} %convolution_bitcast_fusion), channel_id=1, source_target_pairs={{1,2},{3,4},{5,6},{7,8},{9,10},{11,12},{13,14},{2,1},{4,3},{6,5},{... | collective-permute-start | bytes 786440 | tf_op jit(solution)/shard_map/ppermute | solution.py:22
  2.8 11.6 %collective-permute-start = (f32[2,2,128,128]{3,2,1,0:T(8,128)S(1)}, f32[2,2,128,128]{3,2,1,0:T(8,128)S(1)}, u32[]{:S(2)}, u32[]{:S(2)}) collective-permute-start(f32[2,2,128,128]{3,2,1,0:T(8,128)S(1)} %convolution_bitcast_fusion), channel_id=1, source_target_pairs={{0,1},{2,3},{4,5},{6,7},{8,9},{10,11},{12,13},{14,15},{1,0},{3,2},... | collective-permute-start | bytes 786440 | tf_op jit(solution)/shard_map/ppermute | solution.py:22
  14.5 47.0 %collective-permute-start.3 = (f32[2,6,128,128]{3,2,1,0:T(8,128)S(1)}, f32[2,6,128,128]{3,2,1,0:T(8,128)S(1)}, u32[]{:S(2)}, u32[]{:S(2)}) collective-permute-start(f32[2,6,128,128]{3,2,1,0:T(8,128)S(1)} %constant_dynamic-update-slice_fusion.refs_0_), channel_id=1, source_target_pairs={{16,32},{48,64},{80,96},{112,128},{144,160},{176,192},{208,224},{2... | collective-permute-start | bytes 2359304 | tf_op jit(solution)/shard_map/ppermute | solution.py:22
  20.4 41.1 %collective-permute-start.2 = (f32[2,6,128,128]{3,2,1,0:T(8,128)S(1)}, f32[2,6,128,128]{3,2,1,0:T(8,128)S(1)}, u32[]{:S(2)}, u32[]{:S(2)}) collective-permute-start(f32[2,6,128,128]{3,2,1,0:T(8,128)S(1)} %constant_dynamic-update-slice_fusion.refs_0_), channel_id=1, source_target_pairs={{0,16},{32,48},{64,80},{96,112},{128,144},{160,176},{192,208},{224... | collective-permute-start | bytes 2359304 | tf_op jit(solution)/shard_map/ppermute | solution.py:22
  36.9 24.6 %copy-start.1 = (f32[3,128]{1,0:T(4,128)S(1)}, f32[3,128]{1,0:T(4,128)}, u32[]{:S(2)}) copy-start(f32[3,128]{1,0:T(4,128)} %gains.3) | copy-start | bytes 4612
  36.9 24.6 %copy-start.2 = (f32[3,128]{1,0:T(4,128)S(1)}, f32[3,128]{1,0:T(4,128)}, u32[]{:S(2)}) copy-start(f32[3,128]{1,0:T(4,128)} %shifts.3) | copy-start | bytes 4612

commit v6 on v5

--- a/solution.py
+++ b/solution.py
@@ -58,17 +58,25 @@
 
 
 def conv_kernel(norm, count, block, whole, rim, swapped, at, held, gains, shifts, *refs):
-    pieces = 3 if swapped else 1
-    fields, (source, out, stats, gain, moved, stacked, weight, arrived) = refs[:pieces], refs[pieces:]
-    fetch = pltpu.make_async_copy(source, weight, arrived)
-    fetch.start()
+    pieces, results = (3, 2) if swapped else (2, 1)
+    fields, weight, outs, (stats, gain, moved, stacked, *fetching) = (
+        refs[:pieces],
+        refs[pieces],
+        refs[pieces + 1 : pieces + 1 + results],
+        refs[pieces + 1 + results :],
+    )
+    if fetching:
+        source, (weight, arrived) = weight, fetching
+        fetch = pltpu.make_async_copy(source, weight, arrived)
+        fetch.start()
     length, channels = fields[0].shape[2:]
-    rows, depth = len(fields) * fields[0].shape[0], fields[0].shape[1]
+    rows, depth = pieces * fields[0].shape[0], 3 * block[1] if swapped else block[1] + 2
 
     mean, scale, shift = affine(held, count, gains[norm : norm + 1, :], shifts[norm : norm + 1, :])
     row_at = at[0] * block[0] - (rows - block[0]) // 2
     depth_at = at[1] * block[1] - (depth - block[1]) // 2
-    row_groups = orders(at[0], block[0] if swapped else rows, swapped)
+    each = fields[0].shape[0]
+    row_groups = orders(at[0], block[0], True) if swapped else [(i * each, i * each, each) for i in range(pieces)]
     depth_groups = orders(at[1], block[1] if swapped else depth, swapped)
     for piece, (_, to_row, row_count) in enumerate(row_groups):
         for from_cell, to_cell, cell_count in depth_groups:
@@ -82,8 +90,10 @@
                     value = jnp.maximum(value, 0.01 * value)
                     stacked[row * depth + cell] = value.astype(jnp.bfloat16)
 
-    fetch.wait()
+    if fetching:
+        fetch.wait()
     cells = depth - 2
+    out = {row: outs[row * results // (rows - 2)].at[row % ((rows - 2) // results)] for row in range(rows - 2)}
     taps = jnp.concatenate(
         [
             jnp.concatenate(
@@ -113,10 +123,10 @@
             )
             before = jnp.where(place > 0, pltpu.roll(before, 1, 0), 0.0)
             after = jnp.where(place < length - 1, pltpu.roll(after, length - 1, 0), 0.0)
-            out[row, cell] = before + here + after
+            out[row][cell] = before + here + after
 
     inner = [
-        out[row, cell]
+        out[row][cell]
         for row in range(rim, rows - 2 - rim)
         for cell in range(rim, cells - rim)
     ]
@@ -131,30 +141,30 @@
 
 def convolve(norm, count, block, whole, rim, at, held, gains, shifts, fields, weight):
     pieces = len(fields)
-    rows = pieces * fields[0].shape[0]
-    depth, length, channels = fields[0].shape[1:]
+    swapped = pieces == 3
+    each, wide, length, channels = fields[0].shape
+    rows, depth = pieces * each, wide if swapped else block[1] + 2
     in_vmem = pl.BlockSpec(memory_space=pltpu.VMEM)
     flops = 2 * (rows - 2) * (depth - 2) * length * channels * channels * 27
+    row = jax.ShapeDtypeStruct((1, channels), jnp.float32)
+    out = jax.ShapeDtypeStruct((rows - 2, depth - 2, length, channels), jnp.float32)
+    outs = [jax.ShapeDtypeStruct(fields[0].shape, jnp.float32)] * 2 if swapped else [out]
+    outs += [jax.ShapeDtypeStruct((2, channels), jnp.float32), row, row]
+    scratch = [pltpu.VMEM((rows * depth, length, channels), jnp.bfloat16)]
+    if swapped:
+        scratch += [pltpu.VMEM(weight.shape, weight.dtype), pltpu.SemaphoreType.DMA(())]
+        weight = pltpu.with_memory_space_constraint(weight, pltpu.HBM)
     return pl.pallas_call(
-        functools.partial(conv_kernel, norm, count, block, whole, rim, pieces == 3),
-        out_shape=(
-            jax.ShapeDtypeStruct((rows - 2, depth - 2, length, channels), jnp.float32),
-            jax.ShapeDtypeStruct((2, channels), jnp.float32),
-            jax.ShapeDtypeStruct((1, channels), jnp.float32),
-            jax.ShapeDtypeStruct((1, channels), jnp.float32),
-        ),
-        in_specs=[pl.BlockSpec(memory_space=pltpu.SMEM)]
-        + [in_vmem] * (3 + pieces)
-        + [pl.BlockSpec(memory_space=pltpu.HBM)],
-        out_specs=(in_vmem,) * 4,
-        scratch_shapes=[
-            pltpu.VMEM((rows * depth, length, channels), jnp.bfloat16),
-            pltpu.VMEM(weight.shape, weight.dtype),
-            pltpu.SemaphoreType.DMA(()),
-        ],
+        functools.partial(conv_kernel, norm, count, block, whole, rim, swapped),
+        out_shape=outs,
+        in_specs=[pl.BlockSpec(memory_space=pltpu.SMEM)] + [in_vmem] * (3 + pieces)
+        + [pl.BlockSpec(memory_space=pltpu.HBM) if swapped else in_vmem],
+        out_specs=[in_vmem] * len(outs),
+        scratch_shapes=scratch,
+        input_output_aliases={5: 0, 6: 1} if swapped else {},
         compiler_params=pltpu.CompilerParams(vmem_limit_bytes=16 << 20),
         cost_estimate=pl.CostEstimate(flops=flops, bytes_accessed=2 << 20, transcendentals=0),
-    )(at, held, gains, shifts, *fields, pltpu.with_memory_space_constraint(weight, pltpu.HBM))
+    )(at, held, gains, shifts, *fields, weight)
 
 
 def strided(volume, down_weight):
@@ -188,9 +198,9 @@
     wide = jnp.concatenate([coarse] + beside, axis=1)
     beside = swaps(wide, ROWS)
     held = exchanged(stats, DEPTH)
-    middle, stats, _, _ = convolve(0, plane, block, whole, 1, at, held, norm_gain, norm_shift, [wide] + beside, conv_one)
+    upper, lower, stats, _, _ = convolve(0, plane, block, whole, 1, at, held, norm_gain, norm_shift, [wide] + beside, conv_one)
     held = exchanged(pooled(exchanged(stats, ROWS), own), DEPTH)
-    last, stats, gain, shift = convolve(1, plane, block, whole, 0, at, held, norm_gain, norm_shift, [middle], conv_two)
+    last, stats, gain, shift = convolve(1, plane, block, whole, 0, at, held, norm_gain, norm_shift, [upper, lower], conv_two)
     held = exchanged(pooled(exchanged(stats, ROWS), own), DEPTH)
     mean, spread = pooled(held, plane)
     scale = gain[0] / jnp.sqrt(spread / (plane * held.shape[0]) + 1e-05)

time: 123 us -> 122 us (level)
  no operation moved by 1% of the time
where the time goes in v6:
time: 122 us; the launch traced here: 121 us
  blocking collectives  90.8 us (74%)
  starting transfers between devices  15.8 us (13%)
  Pallas kernels  6.93 us (6%)
  waiting for transfers between devices  4.22 us (3%)
  local copies, waits for them, and re-layouts  2.66 us (2%)
    all_to_all x6, blocking collectives, exchanged(): return lax.all_to_all(sent, axis, 0, 0)  90.8 us
    ppermute x4, starting transfers between devices, swaps(): got.append(lax.ppermute(value, axis, pairs + [(j, i) for i, j in pairs]))  15.8 us
    pallas_call x2, Pallas kernels, convolve(): pl.pallas_call(functools.partial(conv_kernel, norm, count, block, whole,...  6.93 us
    ppermute x4, waiting for transfers between devices, swaps(): got.append(lax.ppermute(value, axis, pairs + [(j, i) for i, j in pairs]))  4.22 us
  transfers between devices with their start and end apart: 4, of which 1 were waited for; matrix products, arithmetic and copies ran while one was open for 0% of the time, Pallas kernels for 0%

profile of v6, /device:TPU:1, one launch (start us, length us, event | category | flops | bytes accessed | tf_op | source)
XLA Modules:
  0.0 121.5 jit_solution(10285220760529653805)
XLA Ops:
  0.0 1.7 %copy.47 = bf16[64,4,4,256]{0,3,2,1:T(8,128)(2,1)S(1)} copy(bf16[64,4,4,256]{3,2,1,0:T(4,128)(2,1)} %param.6) | data formatting | bytes 1048576 | tf_op args[0]
  1.7 0.1 pad_add_fusion.at
  1.8 0.4 convolution_bitcast_fusion
  2.1 0.7 collective-permute-start.1
  2.8 7.2 %collective-permute-start = (f32[2,2,128,128]{3,2,1,0:T(8,128)S(1)}, f32[2,2,128,128]{3,2,1,0:T(8,128)S(1)}, u32[]{:S(2)}, u32[]{:S(2)}) collective-permute-start(f32[2,2,128,128]{3,2,1,0:T(8,128)S(1)} %convolution_bitcast_fusion), channel_id=1, source_target_pairs={{0,1},{2,3},{4,5},{6,7},{8,9},{10,11},{12,13},{14,15},{1,0},{3,2},... | collective-permute-start | bytes 786440 | tf_op jit(solution)/shard_map/ppermute | solution.py:22
  10.0 0.1 reduce_sum.90
  10.1 0.1 constant_dynamic-update-slice_fusion.2
  10.2 4.2 %collective-permute-done = f32[2,2,128,128]{3,2,1,0:T(8,128)S(1)} collective-permute-done((f32[2,2,128,128]{3,2,1,0:T(8,128)S(1)}, f32[2,2,128,128]{3,2,1,0:T(8,128)S(1)}, u32[]{:S(2)}, u32[]{:S(2)}) %collective-permute-start) | collective-permute-done | bytes 262176 | tf_op jit(solution)/shard_map/ppermute | solution.py:22
  14.5 5.9 %collective-permute-start.3 = (f32[2,6,128,128]{3,2,1,0:T(8,128)S(1)}, f32[2,6,128,128]{3,2,1,0:T(8,128)S(1)}, u32[]{:S(2)}, u32[]{:S(2)}) collective-permute-start(f32[2,6,128,128]{3,2,1,0:T(8,128)S(1)} %constant_dynamic-update-slice_fusion.refs_0_), channel_id=1, source_target_pairs={{16,32},{48,64},{80,96},{112,128},{144,160},{176,192},{208,224},{2... | collective-permute-start | bytes 2359304 | tf_op jit(solution)/shard_map/ppermute | solution.py:22
  20.4 1.9 %collective-permute-start.2 = (f32[2,6,128,128]{3,2,1,0:T(8,128)S(1)}, f32[2,6,128,128]{3,2,1,0:T(8,128)S(1)}, u32[]{:S(2)}, u32[]{:S(2)}) collective-permute-start(f32[2,6,128,128]{3,2,1,0:T(8,128)S(1)} %constant_dynamic-update-slice_fusion.refs_0_), channel_id=1, source_target_pairs={{0,16},{32,48},{64,80},{96,112},{128,144},{160,176},{192,208},{224... | collective-permute-start | bytes 2359304 | tf_op jit(solution)/shard_map/ppermute | solution.py:22
  22.4 14.4 %all_to_all.30 = f32[32,2,128]{2,1,0:T(2,128)S(1)} all-to-all(f32[32,2,128]{2,1,0:T(2,128)S(1)} %broadcast_in_dim.12), channel_id=1, replica_groups=mesh['x'=4,'y'=4,'core'=2,'z'=16] {'x','y','core'}, dimensions={0} | all-to-all | bytes 65536 | tf_op jit(solution)/shard_map/all_to_all | solution.py:28
  36.9 0.0 copy-start.2
  36.9 0.0 copy-start.3
  36.9 24.6 %all_to_all.31.held = f32[16,2,128]{2,1,0:T(2,128)S(1)} all-to-all(f32[16,2,128]{2,1,0:T(2,128)S(1)} %broadcast_in_dim.13), channel_id=1, replica_groups=mesh['x'=4,'y'=4,'core'=2,'z'=16] {'z'}, dimensions={0} | all-to-all | bytes 32768 | tf_op jit(solution)/shard_map/all_to_all | solution.py:28
  61.5 0.0 collective-permute-done.3.refs_2_
  61.5 0.0 copy-start.1
  61.5 5.4 %shard_map.64 = (f32[2,6,128,128]{3,2,1,0:T(8,128)S(1)}, f32[2,6,128,128]{3,2,1,0:T(8,128)S(1)}, f32[2,128]{1,0:T(2,128)S(1)}, f32[1,128]{1,0:T(1,128)}, f32[1,128]{1,0:T(1,128)}) custom-call(s32[2]{0:T(128)S(1)} %pad_add_fusion.at, f32[16,2,128]{2,1,0:T(2,128)S(1)} %all_to_all.31.held, ...), custom_call_target="tpu_custom_call", output_to_operand_aliasing={{0}: (5, {}), {1}: (6, {})} | custom-call | flops 1811939328 | bytes 2097152 | tf_op jit(solution)/shard_map/pallas_call | solution.py:157
  67.0 12.1 %all_to_all.32 = f32[32,2,128]{2,1,0:T(2,128)S(1)} all-to-all(f32[32,2,128]{2,1,0:T(2,128)S(1)} %broadcast_in_dim.14), channel_id=1, replica_groups=mesh['x'=4,'y'=4,'core'=2,'z'=16] {'x','y','core'}, dimensions={0} | all-to-all | bytes 65536 | tf_op jit(solution)/shard_map/all_to_all | solution.py:28
  79.2 13.9 %all_to_all.33.held = f32[16,2,128]{2,1,0:T(2,128)S(1)} all-to-all(f32[16,2,128]{2,1,0:T(2,128)S(1)} %broadcast_in_dim.15), channel_id=1, replica_groups=mesh['x'=4,'y'=4,'core'=2,'z'=16] {'z'}, dimensions={0} | all-to-all | bytes 32768 | tf_op jit(solution)/shard_map/all_to_all | solution.py:28
  93.1 1.5 %shard_map.65 = (f32[2,2,128,128]{3,2,1,0:T(8,128)S(1)}, f32[2,128]{1,0:T(2,128)S(1)}, f32[1,128]{1,0:T(1,128)S(1)}, f32[1,128]{1,0:T(1,128)S(1)}) custom-call(s32[2]{0:T(128)S(1)} %pad_add_fusion.at, f32[16,2,128]{2,1,0:T(2,128)S(1)} %all_to_all.33.held, f32[3,128]{1,0:T(4,128)S(1)} %copy-done.2, f32[3,128]{1,0:T(4,128)S(1)} %copy-done.3, ...), custom_call_target="tpu_custom_call" | custom-call | flops 452984832 | bytes 2097152 | tf_op jit(solution)/shard_map/pallas_call | solution.py:157
  94.6 11.9 %all_to_all.34 = f32[32,2,128]{2,1,0:T(2,128)S(1)} all-to-all(f32[32,2,128]{2,1,0:T(2,128)S(1)} %broadcast_in_dim.16), channel_id=1, replica_groups=mesh['x'=4,'y'=4,'core'=2,'z'=16] {'x','y','core'}, dimensions={0} | all-to-all | bytes 65536 | tf_op jit(solution)/shard_map/all_to_all | solution.py:28
  106.7 13.9 %all_to_all.35 = f32[16,2,128]{2,1,0:T(2,128)S(1)} all-to-all(f32[16,2,128]{2,1,0:T(2,128)S(1)} %broadcast_in_dim.17), channel_id=1, replica_groups=mesh['x'=4,'y'=4,'core'=2,'z'=16] {'z'}, dimensions={0} | all-to-all | bytes 32768 | tf_op jit(solution)/shard_map/all_to_all | solution.py:28
  120.6 0.1 fusion.2
  120.7 0.8 copy.56
  (37 shorter events, 0.5 us)
Async XLA Ops:
  0.0 1.8 %copy-start = (bf16[128,64,2,2,2]{0,4,3,2,1:T(2,128)(2,1)S(1)}, bf16[128,64,2,2,2]{0,4,3,2,1:T(2,128)(2,1)}, u32[]{:S(2)}) copy-start(bf16[128,64,2,2,2]{0,4,3,2,1:T(2,128)(2,1)} %param.7) | copy-start | bytes 393220
  2.1 12.3 %collective-permute-start.1 = (f32[2,2,128,128]{3,2,1,0:T(8,128)S(1)}, f32[2,2,128,128]{3,2,1,0:T(8,128)S(1)}, u32[]{:S(2)}, u32[]{:S(2)}) collective-permute-start(f32[2,2,128,128]{3,2,1,0:T(8,128)S(1)} %convolution_bitcast_fusion), channel_id=1, source_target_pairs={{1,2},{3,4},{5,6},{7,8},{9,10},{11,12},{13,14},{2,1},{4,3},{6,5},{... | collective-permute-start | bytes 786440 | tf_op jit(solution)/shard_map/ppermute | solution.py:22
  2.8 11.6 %collective-permute-start = (f32[2,2,128,128]{3,2,1,0:T(8,128)S(1)}, f32[2,2,128,128]{3,2,1,0:T(8,128)S(1)}, u32[]{:S(2)}, u32[]{:S(2)}) collective-permute-start(f32[2,2,128,128]{3,2,1,0:T(8,128)S(1)} %convolution_bitcast_fusion), channel_id=1, source_target_pairs={{0,1},{2,3},{4,5},{6,7},{8,9},{10,11},{12,13},{14,15},{1,0},{3,2},... | collective-permute-start | bytes 786440 | tf_op jit(solution)/shard_map/ppermute | solution.py:22
  14.5 47.0 %collective-permute-start.3 = (f32[2,6,128,128]{3,2,1,0:T(8,128)S(1)}, f32[2,6,128,128]{3,2,1,0:T(8,128)S(1)}, u32[]{:S(2)}, u32[]{:S(2)}) collective-permute-start(f32[2,6,128,128]{3,2,1,0:T(8,128)S(1)} %constant_dynamic-update-slice_fusion.refs_0_), channel_id=1, source_target_pairs={{16,32},{48,64},{80,96},{112,128},{144,160},{176,192},{208,224},{2... | collective-permute-start | bytes 2359304 | tf_op jit(solution)/shard_map/ppermute | solution.py:22
  20.4 41.1 %collective-permute-start.2 = (f32[2,6,128,128]{3,2,1,0:T(8,128)S(1)}, f32[2,6,128,128]{3,2,1,0:T(8,128)S(1)}, u32[]{:S(2)}, u32[]{:S(2)}) collective-permute-start(f32[2,6,128,128]{3,2,1,0:T(8,128)S(1)} %constant_dynamic-update-slice_fusion.refs_0_), channel_id=1, source_target_pairs={{0,16},{32,48},{64,80},{96,112},{128,144},{160,176},{192,208},{224... | collective-permute-start | bytes 2359304 | tf_op jit(solution)/shard_map/ppermute | solution.py:22
  36.9 24.6 %copy-start.2 = (f32[3,128]{1,0:T(4,128)S(1)}, f32[3,128]{1,0:T(4,128)}, u32[]{:S(2)}) copy-start(f32[3,128]{1,0:T(4,128)} %gains.3) | copy-start | bytes 4612
  36.9 24.6 %copy-start.3 = (f32[3,128]{1,0:T(4,128)S(1)}, f32[3,128]{1,0:T(4,128)}, u32[]{:S(2)}) copy-start(f32[3,128]{1,0:T(4,128)} %shifts.3) | copy-start | bytes 4612
  61.5 31.6 %copy-start.1 = (bf16[3,3,128,384]{3,2,1,0:T(8,128)(2,1)S(1)}, bf16[3,3,128,384]{3,2,1,0:T(8,128)(2,1)}, u32[]{:S(2)}) copy-start(bf16[3,3,128,384]{3,2,1,0:T(8,128)(2,1)} %refs_2_.1) | copy-start | bytes 2654212
